TPU v7x, 128 devices: a whole 4x4x4 slice. The times are simulated.
128 devices in a mesh: grp: 4 (over z), dp: 2 (over y_hi), mp: 16 (over y_lo, x, core).
Axes of the slice: x: 4, y: 4 (y_hi: 2, y_lo: 2; y = y_hi * 2 + y_lo), z: 4, core: 2. Of those that a mesh axis runs over, the one named last changes fastest.
Arguments:
- tower_features: bfloat16 [4, 4096, 4096], P('grp', 'dp', 'mp'), may hold values from -6 to 6
- doc_weight: bfloat16 [4096, 1024], P('mp'), may hold values from -6 to 6
- query_weight: bfloat16 [4096, 1024], P('mp'), may hold values from -6 to 6
- positive_ids: int32 [4096], replicated, may hold values from 0 to 12287
Outputs:
- loss: float32 [], replicated
- doc_grad: float32 [4096, 1024], P('mp')
- query_grad: float32 [4096, 1024], P('mp')
- feature_grad: bfloat16 [4, 4096, 4096], P('grp', 'dp', 'mp')
All inputs are finite; a program needn't handle non-finite values.
Results may differ from a plain program's by a relative error of at most 0.003.
The roundings to bfloat16 on the way count: a program that leaves them out, or rounds other values in their place, can miss the bound.
Values may be sent and summed in bfloat16 or wider, within the bound.
No kernel may reach another device: no remote copies, remote signals or barrier semaphores. Data moves between devices by JAX's collectives and lax.ppermute only.
A program may use at most 64 MiB of HBM per device.

v0:
```python
import jax
import jax.numpy as jnp
from jax import lax
from jax.sharding import Mesh
from jax.sharding import PartitionSpec as P


MP = ("yl", "x", "c")
Y = ("dp", "yl")
ZY = ("grp", "dp", "yl")

inverse_temp = 200.0
epsilon_norm = 1e-06
dq_unit = 2.0**26
dp_unit = 2.0**17


def fetch(array, axis, step):
    size = lax.axis_size(axis)
    return lax.ppermute(array, axis, [(k, (k - step) % size) for k in range(size)])


def one_way(array, axis, source, target):
    return lax.ppermute(array, axis, [(source, target)])


def turned(array, shift):
    n = array.shape[0]
    return lax.dynamic_slice_in_dim(jnp.concatenate([array, array]), shift, n, 0)


def part(array, index, count):
    size = array.shape[0] // count
    return lax.dynamic_slice_in_dim(array, index * size, size, 0)


def local(tower_features, doc_weight, query_weight, positive_ids):
    z = lax.axis_index("grp")
    yh, yl, x, c = (lax.axis_index(a) for a in ("dp", "yl", "x", "c"))
    y = 2 * yh + yl
    is_query = z == 3
    live = jnp.logical_not(is_query)
    features = tower_features[0]
    weight = jnp.where(is_query, query_weight, doc_weight)
    rows, feats = features.shape
    emb = weight.shape[1]
    per = rows // 16
    total_q = positive_ids.shape[0]

    outer = lax.ppermute(weight, Y, [(k, 3 - k) for k in range(4)])
    other = fetch(weight, "c", 1)
    outer_other = fetch(outer, "c", 1)
    mine = lax.all_to_all(features.reshape(4, rows // 4, feats), ("yl", "c"), 0, 0, tiled=True)
    sources = ((2 * yl + c, weight), (2 * yl + 1 - c, other))
    sources += ((2 - 2 * yl + c, outer), (3 - 2 * yl - c, outer_other))
    partial = sum(
        jnp.dot(
            lax.dynamic_index_in_dim(mine, k, 0, keepdims=False),
            w,
            preferred_element_type=jnp.float32,
        )
        for k, w in sources
    )
    summed = part(partial, x, 4) + sum(
        fetch(part(partial, (x - k) % 4, 4), "x", k) for k in (1, 2, 3)
    )
    row_norms = jnp.sqrt(jnp.sum(summed * summed, axis=-1, keepdims=True) + epsilon_norm)
    unit_rows = summed / row_norms
    embedded = unit_rows.astype(jnp.bfloat16)

    sent = [one_way(embedded, "grp", 3, k) for k in range(3)]
    passages = jnp.stack([embedded] + [fetch(embedded, "x", k) for k in (1, 2, 3)])
    swapped = fetch(passages, "c", 1)
    passages = jnp.stack([passages, swapped], axis=1).reshape(8 * per, emb)
    query = jnp.where(
        is_query, embedded, jnp.where(z == 0, sent[0], jnp.where(z == 1, sent[1], sent[2]))
    )
    around = [fetch(query, Y, k) for k in (1, 2, 3)]
    queries = jnp.stack([query] + around).reshape(4 * per, emb)

    logits = inverse_temp * lax.dot_general(
        queries, passages, (((1,), (1,)), ((), ())), preferred_element_type=jnp.float32
    )
    ids = positive_ids.reshape(2, 2, 2, 4, per)
    ids = lax.dynamic_slice(ids, (0, 0, c, x, 0), (2, 2, 1, 1, per)).reshape(4, per)
    ids = turned(ids, y).reshape(4 * per)
    k = lax.broadcasted_iota(jnp.int32, (8, per), 0)
    i = lax.broadcasted_iota(jnp.int32, (8, per), 1)
    owner = (yl * 2 + (c + k) % 2) * 4 + (x + k // 2) % 4
    column_ids = (z * total_q + yh * rows + owner * per + i).reshape(1, 8 * per)
    hit = ids[:, None] == column_ids
    positive_part = jnp.sum(jnp.where(hit, logits, 0.0), axis=1)
    local_top = jnp.where(live, jnp.max(logits, axis=1), -1e30)
    local_total = jnp.where(live, jnp.sum(jnp.exp(logits - local_top[:, None]), axis=1), 0.0)
    stats = jnp.stack([local_top, local_total, positive_part])
    stats = turned(stats.reshape(3, 4, per).transpose(1, 0, 2), (4 - y) % 4)
    stats = lax.all_to_all(
        jnp.broadcast_to(stats.reshape(1, 12, per), (16, 12, per)), ZY, 0, 0, tiled=True
    ).reshape(16, 4, 3, per)
    top = jnp.max(stats[:, :, 0], axis=0)
    total = jnp.sum(stats[:, :, 1] * jnp.exp(stats[:, :, 0] - top), axis=0)
    lse = top + jnp.log(total)
    loss = jnp.sum(lse - jnp.sum(stats[:, :, 2], axis=0))
    loss = jnp.broadcast_to(loss, (8, 128))
    loss = loss + fetch(loss, "c", 1)
    loss = (loss + fetch(loss, "x", 2)) + (fetch(loss, "x", 1) + fetch(loss, "x", 3))
    loss = loss[0, 0] / total_q
    lse_rows = turned(lse, y).reshape(4 * per)

    probs = jnp.where(live, jnp.exp(logits - lse_rows[:, None]), 0.0)
    dlogit = ((probs - hit.astype(jnp.float32)) / total_q).astype(jnp.bfloat16)
    dquery = jnp.dot(dlogit, passages, preferred_element_type=jnp.float32)
    dpassage = lax.dot_general(
        dlogit, queries, (((0,), (0,)), ((), ())), preferred_element_type=jnp.float32
    )
    dquery, dpassage = lax.optimization_barrier((dquery, dpassage))
    dquery = dquery.reshape(4, per, emb)
    dpassage = dpassage.reshape(4, 2, per, emb)
    dpassage = dpassage[:, 0] + fetch(dpassage[:, 1], "c", 1)
    dq_parts = [
        fetch((dquery[k] * dq_unit).astype(jnp.float16), Y, 4 - k).astype(jnp.float32)
        for k in (1, 2, 3)
    ]
    dp_parts = [
        fetch((dpassage[k] * dp_unit).astype(jnp.float16), "x", 4 - k).astype(jnp.float32)
        for k in (1, 2, 3)
    ]
    dquery = dquery[0] * dq_unit + sum(dq_parts)
    dpassage = dpassage[0] * dp_unit + sum(dp_parts)
    half = dquery.astype(jnp.float16)
    dquery = sum(one_way(half, "grp", k, 3).astype(jnp.float32) for k in range(3))

    grad_emb = inverse_temp * jnp.where(is_query, dquery / dq_unit, dpassage / dp_unit)
    inner = jnp.sum(unit_rows * grad_emb, axis=-1, keepdims=True)
    grad_proj = ((grad_emb - unit_rows * inner) / row_norms).astype(jnp.bfloat16)

    left, right = grad_proj[:, : emb // 2], grad_proj[:, emb // 2 :]
    left = jnp.stack([left, fetch(left, "yl", 1)])
    right = jnp.stack([right] + [fetch(right, "x", k) for k in (1, 2, 3)])
    left = jnp.stack([left] + [fetch(left, "x", k) for k in (1, 2, 3)], axis=1)
    right = jnp.stack([right, fetch(right, "yl", 1)])
    left = jnp.stack([left, fetch(left, "c", 1)]).reshape(rows, emb // 2)
    right = jnp.stack([right, fetch(right, "c", 1)]).reshape(rows, emb // 2)
    placed = features.reshape(2, 2, 4, per, feats)
    placed = jnp.where(yl == 0, placed, placed[::-1]).transpose(1, 0, 2, 3, 4)
    placed = jnp.where(c == 0, placed, placed[::-1]).transpose(2, 0, 1, 3, 4)
    placed = turned(placed, x).transpose(1, 2, 0, 3, 4).reshape(rows, feats)
    weight_part = jnp.concatenate(
        [
            lax.dot_general(
                placed, g, (((0,), (0,)), ((), ())), preferred_element_type=jnp.float32
            )
            for g in (left, right)
        ],
        axis=1,
    )
    back = sum(
        lax.dot_general(g, w, (((1,), (1,)), ((), ())), preferred_element_type=jnp.float32)
        for g, w in ((left, weight[:, : emb // 2]), (right, weight[:, emb // 2 :]))
    ).astype(jnp.bfloat16)
    back = back.reshape(2, 2, 4, per, feats).transpose(2, 0, 1, 3, 4)
    back = turned(back, (4 - x) % 4).transpose(1, 2, 0, 3, 4)
    back = jnp.where(c == 0, back, back[::-1]).transpose(1, 0, 2, 3, 4)
    back = jnp.where(yl == 0, back, back[::-1])
    feature_part = back.reshape(1, rows, feats)

    share = lax.all_to_all(
        weight_part.reshape(8, feats // 8, emb), ("grp", "dp"), 0, 0, tiled=True
    )
    both = jnp.stack([jnp.sum(share[:6], axis=0), share[6] + share[7]]).astype(jnp.bfloat16)
    both = lax.all_to_all(
        jnp.broadcast_to(both[None], (8, *both.shape)), ("grp", "dp"), 0, 0, tiled=True
    )
    doc_grad = both[:, 0].reshape(feats, emb).astype(jnp.float32)
    query_grad = both[:, 1].reshape(feats, emb).astype(jnp.float32)
    return (loss, doc_grad, query_grad, feature_part)


def solution(mesh):
    split = Mesh(
        mesh.devices.reshape(mesh.shape["grp"], mesh.shape["dp"], 2, 4, 2),
        ("grp", "dp", "yl", "x", "c"),
    )
    placed = (P("grp", "dp", MP), P(MP, None), P(MP, None), P())
    return jax.shard_map(
        local,
        mesh=split,
        in_specs=placed,
        out_specs=(P(), P(MP, None), P(MP, None), P("grp", "dp", MP)),
        check_vma=False,
    )
```

profile of v0, /device:TPU:0, one launch (start us, length us, event | category | flops | bytes accessed | tf_op | source)
XLA Modules:
  0.0 243.8 jit_solution(1879443359771922329)
XLA Ops:
  0.7 3.7 %all-to-all-start = ((bf16[4,512,256]{2,1,0:T(8,128)(2,1)}), bf16[4,512,256]{2,1,0:T(8,128)(2,1)S(1)}, u32[]{:S(2)}, u32[]{:S(2)}) async-start(bf16[4,512,256]{2,1,0:T(8,128)(2,1)} %bitcast.189), calls=%async_computation | async-start | bytes 2097152 | tf_op jit(solution)/shard_map/all_to_all | solution.py:53
  4.4 3.9 %collective-permute-start.1 = (bf16[256,1024]{1,0:T(8,128)(2,1)S(1)}, bf16[256,1024]{1,0:T(8,128)(2,1)S(1)}, u32[]{:S(2)}, u32[]{:S(2)}) collective-permute-start(bf16[256,1024]{1,0:T(8,128)(2,1)S(1)} %broadcast_select_fusion), channel_id=1, source_target_pairs={{0,24},{8,16},{16,8},{24,0},{1,25},{9,17},{17,9},{25,1},{2,26},{10... | collective-permute-start | bytes 1572872 | tf_op jit(solution)/shard_map/ppermute | solution.py:50
  8.3 12.2 %collective-permute-done.1 = bf16[256,1024]{1,0:T(8,128)(2,1)S(1)} collective-permute-done((bf16[256,1024]{1,0:T(8,128)(2,1)S(1)}, bf16[256,1024]{1,0:T(8,128)(2,1)S(1)}, u32[]{:S(2)}, u32[]{:S(2)}) %collective-permute-start.1) | collective-permute-done | bytes 524320 | tf_op jit(solution)/shard_map/ppermute | solution.py:50
  25.4 3.0 %collective-permute-start.4 = (f32[128,1024]{1,0:T(8,128)}, f32[128,1024]{1,0:T(8,128)S(1)}, u32[]{:S(2)}, u32[]{:S(2)}) collective-permute-start(f32[128,1024]{1,0:T(8,128)} %get-tuple-element.22), channel_id=1, source_target_pairs={{0,4},{2,6},{4,0},{6,2},{1,5},{3,7},{5,1},{7,3},{8,12},{10,14},{12... | collective-permute-start | bytes 1572872 | tf_op jit(solution)/shard_map/ppermute | solution.py:20
  31.6 10.3 %collective-permute-done.4 = f32[128,1024]{1,0:T(8,128)S(1)} collective-permute-done((f32[128,1024]{1,0:T(8,128)}, f32[128,1024]{1,0:T(8,128)S(1)}, u32[]{:S(2)}, u32[]{:S(2)}) %collective-permute-start.4) | collective-permute-done | bytes 524320 | tf_op jit(solution)/shard_map/ppermute | solution.py:20
  41.9 10.5 %collective-permute-done.5 = f32[128,1024]{1,0:T(8,128)} collective-permute-done((f32[128,1024]{1,0:T(8,128)}, f32[128,1024]{1,0:T(8,128)}, u32[]{:S(2)}, u32[]{:S(2)}) %collective-permute-start.5) | collective-permute-done | bytes 524320 | tf_op jit(solution)/shard_map/ppermute | solution.py:20
  61.3 7.0 %collective-permute-done.12 = bf16[128,1024]{1,0:T(8,128)(2,1)S(1)} collective-permute-done((bf16[128,1024]{1,0:T(8,128)(2,1)S(1)}, bf16[128,1024]{1,0:T(8,128)(2,1)S(1)}, u32[]{:S(2)}, u32[]{:S(2)}) %collective-permute-start.12) | collective-permute-done | bytes 262176 | tf_op jit(solution)/shard_map/ppermute | solution.py:20
  72.0 6.0 %collective-permute-done.6 = bf16[128,1024]{1,0:T(8,128)(2,1)} collective-permute-done((bf16[128,1024]{1,0:T(8,128)(2,1)S(1)}, bf16[128,1024]{1,0:T(8,128)(2,1)}, u32[]{:S(2)}, u32[]{:S(2)}) %collective-permute-start.6) | collective-permute-done | bytes 262176 | tf_op jit(solution)/shard_map/ppermute | solution.py:24
  79.3 4.4 %collective-permute-start.10 = (bf16[128,1024]{1,0:T(8,128)(2,1)S(1)}, bf16[128,1024]{1,0:T(8,128)(2,1)}, u32[]{:S(2)}, u32[]{:S(2)}) collective-permute-start(bf16[128,1024]{1,0:T(8,128)(2,1)S(1)} %select_select_fusion), channel_id=1, source_target_pairs={{0,16},{8,24},{16,0},{24,8},{1,17},{9,25},{17,1},{25,9},{2,18},{10... | collective-permute-start | bytes 786440 | tf_op jit(solution)/shard_map/ppermute | solution.py:20
  83.8 3.4 %collective-permute-done.11 = bf16[128,1024]{1,0:T(8,128)(2,1)} collective-permute-done((bf16[128,1024]{1,0:T(8,128)(2,1)S(1)}, bf16[128,1024]{1,0:T(8,128)(2,1)}, u32[]{:S(2)}, u32[]{:S(2)}) %collective-permute-start.11) | collective-permute-done | bytes 262176 | tf_op jit(solution)/shard_map/ppermute | solution.py:20
  87.2 3.7 %collective-permute-done.10 = bf16[128,1024]{1,0:T(8,128)(2,1)} collective-permute-done((bf16[128,1024]{1,0:T(8,128)(2,1)S(1)}, bf16[128,1024]{1,0:T(8,128)(2,1)}, u32[]{:S(2)}, u32[]{:S(2)}) %collective-permute-start.10) | collective-permute-done | bytes 262176 | tf_op jit(solution)/shard_map/ppermute | solution.py:20
  96.6 13.8 %all_to_all.20 = f32[16,12,128]{2,1,0:T(8,128)S(1)} all-to-all(f32[16,12,128]{2,1,0:T(8,128)S(1)} %broadcast_in_dim.37), channel_id=1, replica_groups=mesh['grp'=4,'dp'=2,'yl'=2,'x'=4,'c'=2] {'grp','dp','yl'}, dimensions={0} | all-to-all | bytes 196608 | tf_op jit(solution)/shard_map/all_to_all | solution.py:97
  111.2 3.1 %fusion.71 = f32[512,1024]{1,0:T(8,128)S(1)} fusion(bf16[1024,1024]{1,0:T(8,128)(2,1)} %bitcast.193, f32[512,1024]{1,0:T(8,128)S(1)} %get-tuple-element.42, f32[512]{0:T(512)S(1)} %fusion.59, s32[1024]{0:T(1024)S(1)} %fusion.52, s32[512]{0:T(512)S(1)} %fusion.58, pred[]{:T(512)S(6)} %not.3), kind=kOutput, calls=%fused_computation.155 | convolution fusion | flops 1077936128 | bytes 6299649 | tf_op jit(solution)/shard_map/dot_general | solution.py:112
  119.7 12.3 %collective-permute-done.20 = f16[128,1024]{1,0:T(8,128)(2,1)S(1)} collective-permute-done((f16[128,1024]{1,0:T(8,128)(2,1)S(1)}, f16[128,1024]{1,0:T(8,128)(2,1)S(1)}, u32[]{:S(2)}, u32[]{:S(2)}) %collective-permute-start.20) | collective-permute-done | bytes 262176 | tf_op jit(solution)/shard_map/ppermute | solution.py:20
  133.6 4.0 %collective-permute-start.23 = (f16[128,1024]{1,0:T(8,128)(2,1)S(1)}, f16[128,1024]{1,0:T(8,128)(2,1)S(1)}, u32[]{:S(2)}, u32[]{:S(2)}) collective-permute-start(f16[128,1024]{1,0:T(8,128)(2,1)S(1)} %add_convert_fusion), channel_id=1, source_target_pairs={{0,96},{1,97},{2,98},{3,99},{4,100},{5,101},{6,102},{7,103},{8,104... | collective-permute-start | bytes 786440 | tf_op jit(solution)/shard_map/ppermute | solution.py:24
  139.4 4.7 %collective-permute-start.29 = (f16[128,1024]{1,0:T(8,128)(2,1)S(1)}, f16[128,1024]{1,0:T(8,128)(2,1)S(1)}, u32[]{:S(2)}, u32[]{:S(2)}) collective-permute-start(f16[128,1024]{1,0:T(8,128)(2,1)S(1)} %get-tuple-element.20), channel_id=1, source_target_pairs={{0,6},{2,0},{4,2},{6,4},{1,7},{3,1},{5,3},{7,5},{8,14},{10,8},{12,... | collective-permute-start | bytes 786440 | tf_op jit(solution)/shard_map/ppermute | solution.py:20
  147.0 3.3 %collective-permute-done.27 = f16[128,1024]{1,0:T(8,128)(2,1)S(1)} collective-permute-done((f16[128,1024]{1,0:T(8,128)(2,1)S(1)}, f16[128,1024]{1,0:T(8,128)(2,1)S(1)}, u32[]{:S(2)}, u32[]{:S(2)}) %collective-permute-start.27) | collective-permute-done | bytes 262176 | tf_op jit(solution)/shard_map/ppermute | solution.py:20
  150.3 4.0 %collective-permute-done.29 = f16[128,1024]{1,0:T(8,128)(2,1)S(1)} collective-permute-done((f16[128,1024]{1,0:T(8,128)(2,1)S(1)}, f16[128,1024]{1,0:T(8,128)(2,1)S(1)}, u32[]{:S(2)}, u32[]{:S(2)}) %collective-permute-start.29) | collective-permute-done | bytes 262176 | tf_op jit(solution)/shard_map/ppermute | solution.py:20
  156.9 3.8 %collective-permute-start.35 = (bf16[128,512]{1,0:T(8,128)(2,1)S(1)}, bf16[128,512]{1,0:T(8,128)(2,1)S(1)}, u32[]{:S(2)}, u32[]{:S(2)}) collective-permute-start(bf16[128,512]{1,0:T(8,128)(2,1)S(1)} %get-tuple-element.39), channel_id=1, source_target_pairs={{0,6},{2,0},{4,2},{6,4},{1,7},{3,1},{5,3},{7,5},{8,14},{10,8},{12,... | collective-permute-start | bytes 393224 | tf_op jit(solution)/shard_map/ppermute | solution.py:20
  171.3 7.3 %collective-permute-done.32 = bf16[2,128,512]{2,1,0:T(8,128)(2,1)S(1)} collective-permute-done((bf16[2,128,512]{2,1,0:T(8,128)(2,1)S(1)}, bf16[2,128,512]{2,1,0:T(8,128)(2,1)S(1)}, u32[]{:S(2)}, u32[]{:S(2)}) %collective-permute-start.32) | collective-permute-done | bytes 262176 | tf_op jit(solution)/shard_map/ppermute | solution.py:20
  192.1 4.4 %all-to-all-start.2 = ((f32[8,32,1024]{2,1,0:T(8,128)}), f32[8,32,1024]{2,1,0:T(8,128)}, u32[]{:S(2)}, u32[]{:S(2)}) async-start(f32[8,32,1024]{2,1,0:T(8,128)} %bitcast.63), calls=%async_computation.2 | async-start | bytes 2097152 | tf_op jit(solution)/shard_map/all_to_all | solution.py:167
  217.9 4.5 %all-to-all-start.3 = ((bf16[8,2,32,1024]{3,2,1,0:T(8,128)(2,1)}), bf16[8,2,32,1024]{3,2,1,0:T(8,128)(2,1)}, u32[]{:S(2)}, u32[]{:S(2)}) async-start(bf16[8,2,32,1024]{3,2,1,0:T(8,128)(2,1)} %broadcast_in_dim.39), calls=%async_computation.3 | async-start | bytes 2097152 | tf_op jit(solution)/shard_map/all_to_all | solution.py:171
  222.3 3.3 %fusion = bf16[2048,256]{1,0:T(8,128)(2,1)} fusion(f32[2048,256]{1,0:T(8,128)S(1)} %fusion.25, bf16[2048,512]{1,0:T(8,128)(2,1)} %bitcast.185, bf16[256,1024]{1,0:T(8,128)(2,1)S(1)} %broadcast_select_fusion), kind=kOutput, calls=%fused_computation.3 | convolution fusion | flops 537919488 | bytes 5505024 | tf_op jit(solution)/shard_map/dot_general | solution.py:158
  229.5 9.6 %all-to-all-done.3 = bf16[8,2,32,1024]{3,2,1,0:T(8,128)(2,1)} async-done(((bf16[8,2,32,1024]{3,2,1,0:T(8,128)(2,1)}), bf16[8,2,32,1024]{3,2,1,0:T(8,128)(2,1)}, u32[]{:S(2)}, u32[]{:S(2)}) %all-to-all-start.3) | async-done | bytes 1048608 | tf_op jit(solution)/shard_map/all_to_all | solution.py:171
  (167 shorter events, 94.4 us)
Async XLA Ops:
  0.7 19.9 %all-to-all-start = ((bf16[4,512,256]{2,1,0:T(8,128)(2,1)}), bf16[4,512,256]{2,1,0:T(8,128)(2,1)S(1)}, u32[]{:S(2)}, u32[]{:S(2)}) async-start(bf16[4,512,256]{2,1,0:T(8,128)(2,1)} %bitcast.189), calls=%async_computation | async-start | bytes 2097152 | tf_op jit(solution)/shard_map/all_to_all | solution.py:53
  4.4 16.1 %collective-permute-start.1 = (bf16[256,1024]{1,0:T(8,128)(2,1)S(1)}, bf16[256,1024]{1,0:T(8,128)(2,1)S(1)}, u32[]{:S(2)}, u32[]{:S(2)}) collective-permute-start(bf16[256,1024]{1,0:T(8,128)(2,1)S(1)} %broadcast_select_fusion), channel_id=1, source_target_pairs={{0,24},{8,16},{16,8},{24,0},{1,25},{9,17},{17,9},{25,1},{2,26},{10... | collective-permute-start | bytes 1572872 | tf_op jit(solution)/shard_map/ppermute | solution.py:50
  8.3 13.1 %collective-permute-start = (bf16[256,1024]{1,0:T(8,128)(2,1)S(1)}, bf16[256,1024]{1,0:T(8,128)(2,1)S(1)}, u32[]{:S(2)}, u32[]{:S(2)}) collective-permute-start(bf16[256,1024]{1,0:T(8,128)(2,1)S(1)} %broadcast_select_fusion), channel_id=1, source_target_pairs={{0,1},{1,0},{2,3},{3,2},{4,5},{5,4},{6,7},{7,6},{8,9},{9,8},{10,11... | collective-permute-start | bytes 1572872 | tf_op jit(solution)/shard_map/ppermute | solution.py:20
  25.4 16.6 %collective-permute-start.4 = (f32[128,1024]{1,0:T(8,128)}, f32[128,1024]{1,0:T(8,128)S(1)}, u32[]{:S(2)}, u32[]{:S(2)}) collective-permute-start(f32[128,1024]{1,0:T(8,128)} %get-tuple-element.22), channel_id=1, source_target_pairs={{0,4},{2,6},{4,0},{6,2},{1,5},{3,7},{5,1},{7,3},{8,12},{10,14},{12... | collective-permute-start | bytes 1572872 | tf_op jit(solution)/shard_map/ppermute | solution.py:20
  28.4 24.0 %collective-permute-start.5 = (f32[128,1024]{1,0:T(8,128)}, f32[128,1024]{1,0:T(8,128)}, u32[]{:S(2)}, u32[]{:S(2)}) collective-permute-start(f32[128,1024]{1,0:T(8,128)} %get-tuple-element.23), channel_id=1, source_target_pairs={{0,2},{2,4},{4,6},{6,0},{1,3},{3,5},{5,7},{7,1},{8,10},{10,12},{12... | collective-permute-start | bytes 1572872 | tf_op jit(solution)/shard_map/ppermute | solution.py:20
  29.0 23.5 %collective-permute-start.3 = (f32[128,1024]{1,0:T(8,128)}, f32[128,1024]{1,0:T(8,128)}, u32[]{:S(2)}, u32[]{:S(2)}) collective-permute-start(f32[128,1024]{1,0:T(8,128)} %get-tuple-element.24), channel_id=1, source_target_pairs={{0,6},{2,0},{4,2},{6,4},{1,7},{3,1},{5,3},{7,5},{8,14},{10,8},{12,... | collective-permute-start | bytes 1572872 | tf_op jit(solution)/shard_map/ppermute | solution.py:20
  54.2 14.1 %collective-permute-start.12 = (bf16[128,1024]{1,0:T(8,128)(2,1)S(1)}, bf16[128,1024]{1,0:T(8,128)(2,1)S(1)}, u32[]{:S(2)}, u32[]{:S(2)}) collective-permute-start(bf16[128,1024]{1,0:T(8,128)(2,1)S(1)} %fusion.64), channel_id=1, source_target_pairs={{0,6},{2,0},{4,2},{6,4},{1,7},{3,1},{5,3},{7,5},{8,14},{10,8},{12,... | collective-permute-start | bytes 786440 | tf_op jit(solution)/shard_map/ppermute | solution.py:20
  56.9 14.8 %collective-permute-start.14 = (bf16[128,1024]{1,0:T(8,128)(2,1)S(1)}, bf16[128,1024]{1,0:T(8,128)(2,1)S(1)}, u32[]{:S(2)}, u32[]{:S(2)}) collective-permute-start(bf16[128,1024]{1,0:T(8,128)(2,1)S(1)} %fusion.64), channel_id=1, source_target_pairs={{0,2},{2,4},{4,6},{6,0},{1,3},{3,5},{5,7},{7,1},{8,10},{10,12},{12... | collective-permute-start | bytes 786440 | tf_op jit(solution)/shard_map/ppermute | solution.py:20
  56.9 14.8 %collective-permute-start.13 = (bf16[128,1024]{1,0:T(8,128)(2,1)S(1)}, bf16[128,1024]{1,0:T(8,128)(2,1)S(1)}, u32[]{:S(2)}, u32[]{:S(2)}) collective-permute-start(bf16[128,1024]{1,0:T(8,128)(2,1)S(1)} %fusion.64), channel_id=1, source_target_pairs={{0,4},{2,6},{4,0},{6,2},{1,5},{3,7},{5,1},{7,3},{8,12},{10,14},{12... | collective-permute-start | bytes 786440 | tf_op jit(solution)/shard_map/ppermute | solution.py:20
  58.4 13.6 %collective-permute-start.8 = (bf16[128,1024]{1,0:T(8,128)(2,1)S(1)}, bf16[128,1024]{1,0:T(8,128)(2,1)}, u32[]{:S(2)}, u32[]{:S(2)}) collective-permute-start(bf16[128,1024]{1,0:T(8,128)(2,1)S(1)} %fusion.64), channel_id=1, source_target_pairs={{96,64},{97,65},{98,66},{99,67},{100,68},{101,69},{102,70},{103,71... | collective-permute-start | bytes 786440 | tf_op jit(solution)/shard_map/ppermute | solution.py:24
  59.8 12.2 %collective-permute-start.7 = (bf16[128,1024]{1,0:T(8,128)(2,1)S(1)}, bf16[128,1024]{1,0:T(8,128)(2,1)}, u32[]{:S(2)}, u32[]{:S(2)}) collective-permute-start(bf16[128,1024]{1,0:T(8,128)(2,1)S(1)} %fusion.64), channel_id=1, source_target_pairs={{96,32},{97,33},{98,34},{99,35},{100,36},{101,37},{102,38},{103,39... | collective-permute-start | bytes 786440 | tf_op jit(solution)/shard_map/ppermute | solution.py:24
  71.8 20.4 %collective-permute-start.15 = (bf16[4,128,1024]{2,1,0:T(8,128)(2,1)S(1)}, bf16[4,128,1024]{2,1,0:T(8,128)(2,1)}, u32[]{:S(2)}, u32[]{:S(2)}) collective-permute-start(bf16[4,128,1024]{2,1,0:T(8,128)(2,1)S(1)} %get-tuple-element.32), channel_id=1, source_target_pairs={{0,1},{1,0},{2,3},{3,2},{4,5},{5,4},{6,7},{7,6},{8,9},{9,8},{10,11... | collective-permute-start | bytes 3145736 | tf_op jit(solution)/shard_map/ppermute | solution.py:20
  116.1 21.4 %collective-permute-start.26 = (f32[4,128,1024]{2,1,0:T(8,128)S(1)}, f32[4,128,1024]{2,1,0:T(8,128)S(1)}, u32[]{:S(2)}, u32[]{:S(2)}) collective-permute-start(f32[4,128,1024]{2,1,0:T(8,128)S(1)} %slice_bitcast_fusion), channel_id=1, source_target_pairs={{0,1},{1,0},{2,3},{3,2},{4,5},{5,4},{6,7},{7,6},{8,9},{9,8},{10,11... | collective-permute-start | bytes 6291464 | tf_op jit(solution)/shard_map/ppermute | solution.py:20
  116.4 15.6 %collective-permute-start.20 = (f16[128,1024]{1,0:T(8,128)(2,1)S(1)}, f16[128,1024]{1,0:T(8,128)(2,1)S(1)}, u32[]{:S(2)}, u32[]{:S(2)}) collective-permute-start(f16[128,1024]{1,0:T(8,128)(2,1)S(1)} %get-tuple-element.16), channel_id=1, source_target_pairs={{0,8},{8,16},{16,24},{24,0},{1,9},{9,17},{17,25},{25,1},{2,10},{10... | collective-permute-start | bytes 786440 | tf_op jit(solution)/shard_map/ppermute | solution.py:20
  117.0 15.0 %collective-permute-start.22 = (f16[128,1024]{1,0:T(8,128)(2,1)S(1)}, f16[128,1024]{1,0:T(8,128)(2,1)S(1)}, u32[]{:S(2)}, u32[]{:S(2)}) collective-permute-start(f16[128,1024]{1,0:T(8,128)(2,1)S(1)} %get-tuple-element.17), channel_id=1, source_target_pairs={{0,24},{8,0},{16,8},{24,16},{1,25},{9,1},{17,9},{25,17},{2,26},{10... | collective-permute-start | bytes 786440 | tf_op jit(solution)/shard_map/ppermute | solution.py:20
  119.7 12.3 %collective-permute-start.21 = (f16[128,1024]{1,0:T(8,128)(2,1)S(1)}, f16[128,1024]{1,0:T(8,128)(2,1)S(1)}, u32[]{:S(2)}, u32[]{:S(2)}) collective-permute-start(f16[128,1024]{1,0:T(8,128)(2,1)S(1)} %get-tuple-element.18), channel_id=1, source_target_pairs={{0,16},{8,24},{16,0},{24,8},{1,17},{9,25},{17,1},{25,9},{2,18},{10... | collective-permute-start | bytes 786440 | tf_op jit(solution)/shard_map/ppermute | solution.py:20
  132.9 12.6 %collective-permute-start.24 = (f16[128,1024]{1,0:T(8,128)(2,1)S(1)}, f16[128,1024]{1,0:T(8,128)(2,1)S(1)}, u32[]{:S(2)}, u32[]{:S(2)}) collective-permute-start(f16[128,1024]{1,0:T(8,128)(2,1)S(1)} %add_convert_fusion), channel_id=1, source_target_pairs={{32,96},{33,97},{34,98},{35,99},{36,100},{37,101},{38,102},{39,103... | collective-permute-start | bytes 786440 | tf_op jit(solution)/shard_map/ppermute | solution.py:24
  133.6 13.5 %collective-permute-start.23 = (f16[128,1024]{1,0:T(8,128)(2,1)S(1)}, f16[128,1024]{1,0:T(8,128)(2,1)S(1)}, u32[]{:S(2)}, u32[]{:S(2)}) collective-permute-start(f16[128,1024]{1,0:T(8,128)(2,1)S(1)} %add_convert_fusion), channel_id=1, source_target_pairs={{0,96},{1,97},{2,98},{3,99},{4,100},{5,101},{6,102},{7,103},{8,104... | collective-permute-start | bytes 786440 | tf_op jit(solution)/shard_map/ppermute | solution.py:24
  138.3 12.0 %collective-permute-start.27 = (f16[128,1024]{1,0:T(8,128)(2,1)S(1)}, f16[128,1024]{1,0:T(8,128)(2,1)S(1)}, u32[]{:S(2)}, u32[]{:S(2)}) collective-permute-start(f16[128,1024]{1,0:T(8,128)(2,1)S(1)} %get-tuple-element.19), channel_id=1, source_target_pairs={{0,2},{2,4},{4,6},{6,0},{1,3},{3,5},{5,7},{7,1},{8,10},{10,12},{12... | collective-permute-start | bytes 786440 | tf_op jit(solution)/shard_map/ppermute | solution.py:20
  139.4 14.9 %collective-permute-start.29 = (f16[128,1024]{1,0:T(8,128)(2,1)S(1)}, f16[128,1024]{1,0:T(8,128)(2,1)S(1)}, u32[]{:S(2)}, u32[]{:S(2)}) collective-permute-start(f16[128,1024]{1,0:T(8,128)(2,1)S(1)} %get-tuple-element.20), channel_id=1, source_target_pairs={{0,6},{2,0},{4,2},{6,4},{1,7},{3,1},{5,3},{7,5},{8,14},{10,8},{12,... | collective-permute-start | bytes 786440 | tf_op jit(solution)/shard_map/ppermute | solution.py:20
  144.1 12.0 %collective-permute-start.28 = (f16[128,1024]{1,0:T(8,128)(2,1)S(1)}, f16[128,1024]{1,0:T(8,128)(2,1)S(1)}, u32[]{:S(2)}, u32[]{:S(2)}) collective-permute-start(f16[128,1024]{1,0:T(8,128)(2,1)S(1)} %get-tuple-element.21), channel_id=1, source_target_pairs={{0,4},{2,6},{4,0},{6,2},{1,5},{3,7},{5,1},{7,3},{8,12},{10,14},{12... | collective-permute-start | bytes 786440 | tf_op jit(solution)/shard_map/ppermute | solution.py:20
  167.0 15.9 %collective-permute-start.38 = (bf16[4,128,512]{2,1,0:T(8,128)(2,1)S(1)}, bf16[4,128,512]{2,1,0:T(8,128)(2,1)S(1)}, u32[]{:S(2)}, u32[]{:S(2)}) collective-permute-start(bf16[4,128,512]{2,1,0:T(8,128)(2,1)S(1)} %get-tuple-element.34), channel_id=1, source_target_pairs={{0,8},{8,0},{1,9},{9,1},{2,10},{10,2},{3,11},{11,3},{4,12},{12,4},... | collective-permute-start | bytes 1572872 | tf_op jit(solution)/shard_map/ppermute | solution.py:20
  192.1 22.5 %all-to-all-start.2 = ((f32[8,32,1024]{2,1,0:T(8,128)}), f32[8,32,1024]{2,1,0:T(8,128)}, u32[]{:S(2)}, u32[]{:S(2)}) async-start(f32[8,32,1024]{2,1,0:T(8,128)} %bitcast.63), calls=%async_computation.2 | async-start | bytes 2097152 | tf_op jit(solution)/shard_map/all_to_all | solution.py:167
  217.9 21.2 %all-to-all-start.3 = ((bf16[8,2,32,1024]{3,2,1,0:T(8,128)(2,1)}), bf16[8,2,32,1024]{3,2,1,0:T(8,128)(2,1)}, u32[]{:S(2)}, u32[]{:S(2)}) async-start(bf16[8,2,32,1024]{3,2,1,0:T(8,128)(2,1)} %broadcast_in_dim.39), calls=%async_computation.3 | async-start | bytes 2097152 | tf_op jit(solution)/shard_map/all_to_all | solution.py:171
  (32 other events, 208.6 us)
where the time goes:
time: 245 us; the launch traced here: 244 us
  waiting for transfers between devices  111 us (45%)
  starting transfers between devices  64.2 us (26%)
  other arithmetic  25 us (10%)
  matrix products  17.1 us (7%)
  blocking collectives  13.8 us (6%)
  local copies, waits for them, and re-layouts  9.63 us (4%)
  between operations  3.13 us (1%)
    ppermute x33, waiting for transfers between devices, fetch(): lax.ppermute(array, axis, [(k, (k - step) % size) for k in range(size)])  78.9 us
    ppermute x33, starting transfers between devices, fetch(): lax.ppermute(array, axis, [(k, (k - step) % size) for k in range(size)])  38.3 us
    all_to_all x1, blocking collectives, local(): lax.all_to_all(jnp.broadcast_to(stats.reshape(1, 12, per), (16, 12, per))...  13.8 us
    ppermute x1, waiting for transfers between devices, local(): outer = lax.ppermute(weight, Y, [(k, 3 - k) for k in range(4)])  12.2 us
    all_to_all x1, waiting for transfers between devices, local(): lax.all_to_all(jnp.broadcast_to(both[None], (8, *both.shape)), ('grp', 'd...  9.57 us
    ppermute x6, starting transfers between devices, one_way(): return lax.ppermute(array, axis, [(source, target)])  9.37 us
    ppermute x6, waiting for transfers between devices, one_way(): return lax.ppermute(array, axis, [(source, target)])  7.55 us
  transfers between devices with their start and end apart: 43, of which 26 were waited for; matrix products, arithmetic and copies ran while one was open for 12% of the time, Pallas kernels for 0%

commit v1 on v0

--- a/solution.py
+++ b/solution.py
@@ -1,6 +1,8 @@
 import jax
 import jax.numpy as jnp
 from jax import lax
+from jax.experimental import pallas as pl
+from jax.experimental.pallas import tpu as pltpu
 from jax.sharding import Mesh
 from jax.sharding import PartitionSpec as P
 
@@ -32,6 +34,83 @@
 def part(array, index, count):
     size = array.shape[0] // count
     return lax.dynamic_slice_in_dim(array, index * size, size, 0)
+
+
+def row_order_kernel(at, *refs):
+    *pieces, out = refs
+    lefts, rights = pieces[:8], pieces[8:]
+    per, half = lefts[0].shape[1:]
+
+    def rows(side, core, along):
+        block = ((at[0] + side) % 2 * 2 + (at[1] + core) % 2) * 4 + (at[2] + along) % 4
+        return pl.ds(pl.multiple_of(block * per, per), per)
+
+    for core in range(2):
+        for side in range(2):
+            for k in range(4):
+                out[rows(side, core, k), :half] = lefts[core * 4 + k][side]
+                out[rows(side, core, k), half:] = rights[core * 2 + side][k]
+
+
+def in_row_order(at, lefts, rights):
+    per, half = lefts[0].shape[1:]
+    vmem = pl.BlockSpec(memory_space=pltpu.VMEM)
+    return pl.pallas_call(
+        row_order_kernel,
+        out_shape=jax.ShapeDtypeStruct((16 * per, 2 * half), lefts[0].dtype),
+        in_specs=[pl.BlockSpec(memory_space=pltpu.SMEM)] + [vmem] * 12,
+        out_specs=vmem,
+        cost_estimate=pl.CostEstimate(
+            flops=0, bytes_accessed=64 * per * half * 2, transcendentals=0
+        ),
+        compiler_params=pltpu.CompilerParams(vmem_limit_bytes=12 * 2**20),
+    )(at, *lefts, *rights)
+
+
+def summed_copies_kernel(share, out):
+    doc = ((share[0] + share[1]) + (share[2] + share[3])) + (share[4] + share[5])
+    doc = doc.astype(out.dtype)
+    query = (share[6] + share[7]).astype(out.dtype)
+    for k in range(8):
+        out[k, 0] = doc
+        out[k, 1] = query
+
+
+def summed_copies(share):
+    vmem = pl.BlockSpec(memory_space=pltpu.VMEM)
+    n, rows, emb = share.shape
+    return pl.pallas_call(
+        summed_copies_kernel,
+        out_shape=jax.ShapeDtypeStruct((n, 2, rows, emb), jnp.bfloat16),
+        in_specs=[vmem],
+        out_specs=vmem,
+        cost_estimate=pl.CostEstimate(
+            flops=share.size, bytes_accessed=share.size * 8, transcendentals=0
+        ),
+        compiler_params=pltpu.CompilerParams(vmem_limit_bytes=6 * 2**20),
+    )(share)
+
+
+def widened_kernel(both, doc, query):
+    n, _, rows, _ = both.shape
+    for k in range(n):
+        doc[k * rows : (k + 1) * rows, :] = both[k, 0].astype(jnp.float32)
+        query[k * rows : (k + 1) * rows, :] = both[k, 1].astype(jnp.float32)
+
+
+def widened(both):
+    vmem = pl.BlockSpec(memory_space=pltpu.VMEM)
+    n, _, rows, emb = both.shape
+    return pl.pallas_call(
+        widened_kernel,
+        out_shape=[jax.ShapeDtypeStruct((n * rows, emb), jnp.float32)] * 2,
+        in_specs=[vmem],
+        out_specs=[vmem] * 2,
+        cost_estimate=pl.CostEstimate(
+            flops=0, bytes_accessed=both.size * 6, transcendentals=0
+        ),
+        compiler_params=pltpu.CompilerParams(vmem_limit_bytes=6 * 2**20),
+    )(both)
 
 
 def local(tower_features, doc_weight, query_weight, positive_ids):
@@ -103,7 +182,8 @@
     loss = jnp.sum(lse - jnp.sum(stats[:, :, 2], axis=0))
     loss = jnp.broadcast_to(loss, (8, 128))
     loss = loss + fetch(loss, "c", 1)
-    loss = (loss + fetch(loss, "x", 2)) + (fetch(loss, "x", 1) + fetch(loss, "x", 3))
+    losses = [fetch(loss, "x", k) for k in (1, 2, 3)]
+    loss = (loss + losses[1]) + (losses[0] + losses[2])
     loss = loss[0, 0] / total_q
     lse_rows = turned(lse, y).reshape(4 * per)
 
@@ -137,42 +217,23 @@
     left, right = grad_proj[:, : emb // 2], grad_proj[:, emb // 2 :]
     left = jnp.stack([left, fetch(left, "yl", 1)])
     right = jnp.stack([right] + [fetch(right, "x", k) for k in (1, 2, 3)])
-    left = jnp.stack([left] + [fetch(left, "x", k) for k in (1, 2, 3)], axis=1)
-    right = jnp.stack([right, fetch(right, "yl", 1)])
-    left = jnp.stack([left, fetch(left, "c", 1)]).reshape(rows, emb // 2)
-    right = jnp.stack([right, fetch(right, "c", 1)]).reshape(rows, emb // 2)
-    placed = features.reshape(2, 2, 4, per, feats)
-    placed = jnp.where(yl == 0, placed, placed[::-1]).transpose(1, 0, 2, 3, 4)
-    placed = jnp.where(c == 0, placed, placed[::-1]).transpose(2, 0, 1, 3, 4)
-    placed = turned(placed, x).transpose(1, 2, 0, 3, 4).reshape(rows, feats)
-    weight_part = jnp.concatenate(
-        [
-            lax.dot_general(
-                placed, g, (((0,), (0,)), ((), ())), preferred_element_type=jnp.float32
-            )
-            for g in (left, right)
-        ],
-        axis=1,
-    )
-    back = sum(
-        lax.dot_general(g, w, (((1,), (1,)), ((), ())), preferred_element_type=jnp.float32)
-        for g, w in ((left, weight[:, : emb // 2]), (right, weight[:, emb // 2 :]))
-    ).astype(jnp.bfloat16)
-    back = back.reshape(2, 2, 4, per, feats).transpose(2, 0, 1, 3, 4)
-    back = turned(back, (4 - x) % 4).transpose(1, 2, 0, 3, 4)
-    back = jnp.where(c == 0, back, back[::-1]).transpose(1, 0, 2, 3, 4)
-    back = jnp.where(yl == 0, back, back[::-1])
-    feature_part = back.reshape(1, rows, feats)
+    lefts = [left] + [fetch(left, "x", k) for k in (1, 2, 3)]
+    rights = [right, fetch(right, "yl", 1)]
+    lefts += [fetch(p, "c", 1) for p in lefts]
+    rights += [fetch(p, "c", 1) for p in rights]
+    gathered = in_row_order(jnp.stack([yl, c, x]), lefts, rights)
+    weight_part = lax.dot_general(
+        features, gathered, (((0,), (0,)), ((), ())), preferred_element_type=jnp.float32
+    )
+    feature_part = lax.dot_general(
+        gathered, weight, (((1,), (1,)), ((), ())), preferred_element_type=jnp.float32
+    ).astype(jnp.bfloat16)[None]
 
     share = lax.all_to_all(
         weight_part.reshape(8, feats // 8, emb), ("grp", "dp"), 0, 0, tiled=True
     )
-    both = jnp.stack([jnp.sum(share[:6], axis=0), share[6] + share[7]]).astype(jnp.bfloat16)
-    both = lax.all_to_all(
-        jnp.broadcast_to(both[None], (8, *both.shape)), ("grp", "dp"), 0, 0, tiled=True
-    )
-    doc_grad = both[:, 0].reshape(feats, emb).astype(jnp.float32)
-    query_grad = both[:, 1].reshape(feats, emb).astype(jnp.float32)
+    both = lax.all_to_all(summed_copies(share), ("grp", "dp"), 0, 0, tiled=True)
+    doc_grad, query_grad = widened(both)
     return (loss, doc_grad, query_grad, feature_part)
 
 

time: 245 us -> 249 us (1.016)
  blocking collectives: 13.8 us -> 35.5 us
  other arithmetic: 25 us -> 11 us
  local copies, waits for them, and re-layouts: 9.63 us -> 3.64 us
  waiting for transfers between devices: 111 us -> 116 us
  starting transfers between devices: 64.2 us -> 60.5 us
  Pallas kernels: 0 us -> 3.33 us
    all_to_all x0 -> x1, blocking collectives: none -> 21.7 us  [local(): lax.all_to_all(weight_part.reshape(8, feats // 8, emb), ('grp', 'dp'), 0,...]
    ppermute x33 -> x37, waiting for transfers between devices: 78.9 us -> 95.7 us  [fetch(): lax.ppermute(array, axis, [(k, (k - step) % size) for k in range(size)])]
    all_to_all x2 -> x1, waiting for transfers between devices: 12.3 us -> 0.01 us  [local(): both = lax.all_to_all(summed_copies(share), ('grp', 'dp'), 0, 0, tiled=True)]
    another operation x8 -> x3, other arithmetic: 8.25 us -> 0.17 us  [the longest x1 0.08 us: local(): gathered = in_row_order(jnp.stack([yl, c, x]), lefts, rights)]
    all_to_all x2 -> x1, starting transfers between devices: 8.89 us -> 3.56 us  [local(): both = lax.all_to_all(summed_copies(share), ('grp', 'dp'), 0, 0, tiled=True)]
    pallas_call x0 -> x3, Pallas kernels: none -> 3.33 us  [the longest x1 1.44 us: widened(): pl.pallas_call(widened_kernel, out_shape=[jax.ShapeDtypeStruct((n * rows,...]
    dot_general x4 -> x2, matrix products: 8.06 us -> 5.76 us  [the longest x1 4.45 us: local(): lax.dot_general(gathered, weight, (((1,), (1,)), ((), ())), preferred_ele...]
    ppermute x33 -> x37, starting transfers between devices: 38.3 us -> 40 us  [fetch(): lax.ppermute(array, axis, [(k, (k - step) % size) for k in range(size)])]
  transfers between devices with their start and end apart: 43 -> 46, of which waited for: 26 -> 28; matrix products, arithmetic and copies ran while one was open for 12% -> 5% of each run, Pallas kernels for 0% -> 0%
where the time goes in v1:
time: 249 us; the launch traced here: 247 us
  waiting for transfers between devices  116 us (47%)
  starting transfers between devices  60.5 us (24%)
  blocking collectives  35.5 us (14%)
  matrix products  14.8 us (6%)
  other arithmetic  11 us (4%)
  local copies, waits for them, and re-layouts  3.64 us (1%)
  Pallas kernels  3.33 us (1%)
  between operations  3.01 us (1%)
    ppermute x37, waiting for transfers between devices, fetch(): lax.ppermute(array, axis, [(k, (k - step) % size) for k in range(size)])  95.7 us
    ppermute x37, starting transfers between devices, fetch(): lax.ppermute(array, axis, [(k, (k - step) % size) for k in range(size)])  40 us
    all_to_all x1, blocking collectives, local(): lax.all_to_all(weight_part.reshape(8, feats // 8, emb), ('grp', 'dp'), 0,...  21.7 us
    all_to_all x1, blocking collectives, local(): lax.all_to_all(jnp.broadcast_to(stats.reshape(1, 12, per), (16, 12, per))...  13.8 us
    ppermute x1, waiting for transfers between devices, local(): outer = lax.ppermute(weight, Y, [(k, 3 - k) for k in range(4)])  12.2 us
    ppermute x6, starting transfers between devices, one_way(): return lax.ppermute(array, axis, [(source, target)])  9.36 us
    ppermute x6, waiting for transfers between devices, one_way(): return lax.ppermute(array, axis, [(source, target)])  7.57 us
  transfers between devices with their start and end apart: 46, of which 28 were waited for; matrix products, arithmetic and copies ran while one was open for 5% of the time, Pallas kernels for 0%

profile of v1, /device:TPU:0, one launch (start us, length us, event | category | flops | bytes accessed | tf_op | source)
XLA Modules:
  0.0 247.3 jit_solution(7762241318710248686)
XLA Ops:
  0.7 3.7 %all-to-all-start = ((bf16[4,512,256]{2,1,0:T(8,128)(2,1)}), bf16[4,512,256]{2,1,0:T(8,128)(2,1)S(1)}, u32[]{:S(2)}, u32[]{:S(2)}) async-start(bf16[4,512,256]{2,1,0:T(8,128)(2,1)} %bitcast.150), calls=%async_computation | async-start | bytes 2097152 | tf_op jit(solution)/shard_map/all_to_all | solution.py:132
  4.4 3.9 %collective-permute-start.1 = (bf16[256,1024]{1,0:T(8,128)(2,1)S(1)}, bf16[256,1024]{1,0:T(8,128)(2,1)S(1)}, u32[]{:S(2)}, u32[]{:S(2)}) collective-permute-start(bf16[256,1024]{1,0:T(8,128)(2,1)S(1)} %broadcast_select_fusion), channel_id=1, source_target_pairs={{0,24},{8,16},{16,8},{24,0},{1,25},{9,17},{17,9},{25,1},{2,26},{10... | collective-permute-start | bytes 1572872 | tf_op jit(solution)/shard_map/ppermute | solution.py:129
  8.3 12.2 %collective-permute-done.1 = bf16[256,1024]{1,0:T(8,128)(2,1)S(1)} collective-permute-done((bf16[256,1024]{1,0:T(8,128)(2,1)S(1)}, bf16[256,1024]{1,0:T(8,128)(2,1)S(1)}, u32[]{:S(2)}, u32[]{:S(2)}) %collective-permute-start.1) | collective-permute-done | bytes 524320 | tf_op jit(solution)/shard_map/ppermute | solution.py:129
  31.6 10.3 %collective-permute-done.4 = f32[128,1024]{1,0:T(8,128)S(1)} collective-permute-done((f32[128,1024]{1,0:T(8,128)}, f32[128,1024]{1,0:T(8,128)S(1)}, u32[]{:S(2)}, u32[]{:S(2)}) %collective-permute-start.4) | collective-permute-done | bytes 524320 | tf_op jit(solution)/shard_map/ppermute | solution.py:22
  41.9 10.5 %collective-permute-done.5 = f32[128,1024]{1,0:T(8,128)} collective-permute-done((f32[128,1024]{1,0:T(8,128)}, f32[128,1024]{1,0:T(8,128)}, u32[]{:S(2)}, u32[]{:S(2)}) %collective-permute-start.5) | collective-permute-done | bytes 524320 | tf_op jit(solution)/shard_map/ppermute | solution.py:22
  61.3 7.0 %collective-permute-done.12 = bf16[128,1024]{1,0:T(8,128)(2,1)S(1)} collective-permute-done((bf16[128,1024]{1,0:T(8,128)(2,1)S(1)}, bf16[128,1024]{1,0:T(8,128)(2,1)S(1)}, u32[]{:S(2)}, u32[]{:S(2)}) %collective-permute-start.12) | collective-permute-done | bytes 262176 | tf_op jit(solution)/shard_map/ppermute | solution.py:22
  72.0 6.0 %collective-permute-done.6 = bf16[128,1024]{1,0:T(8,128)(2,1)} collective-permute-done((bf16[128,1024]{1,0:T(8,128)(2,1)S(1)}, bf16[128,1024]{1,0:T(8,128)(2,1)}, u32[]{:S(2)}, u32[]{:S(2)}) %collective-permute-start.6) | collective-permute-done | bytes 262176 | tf_op jit(solution)/shard_map/ppermute | solution.py:26
  79.3 4.4 %collective-permute-start.10 = (bf16[128,1024]{1,0:T(8,128)(2,1)S(1)}, bf16[128,1024]{1,0:T(8,128)(2,1)}, u32[]{:S(2)}, u32[]{:S(2)}) collective-permute-start(bf16[128,1024]{1,0:T(8,128)(2,1)S(1)} %select_select_fusion), channel_id=1, source_target_pairs={{0,16},{8,24},{16,0},{24,8},{1,17},{9,25},{17,1},{25,9},{2,18},{10... | collective-permute-start | bytes 786440 | tf_op jit(solution)/shard_map/ppermute | solution.py:22
  83.8 3.4 %collective-permute-done.11 = bf16[128,1024]{1,0:T(8,128)(2,1)} collective-permute-done((bf16[128,1024]{1,0:T(8,128)(2,1)S(1)}, bf16[128,1024]{1,0:T(8,128)(2,1)}, u32[]{:S(2)}, u32[]{:S(2)}) %collective-permute-start.11) | collective-permute-done | bytes 262176 | tf_op jit(solution)/shard_map/ppermute | solution.py:22
  87.2 3.7 %collective-permute-done.10 = bf16[128,1024]{1,0:T(8,128)(2,1)} collective-permute-done((bf16[128,1024]{1,0:T(8,128)(2,1)S(1)}, bf16[128,1024]{1,0:T(8,128)(2,1)}, u32[]{:S(2)}, u32[]{:S(2)}) %collective-permute-start.10) | collective-permute-done | bytes 262176 | tf_op jit(solution)/shard_map/ppermute | solution.py:22
  96.6 13.8 %all_to_all.20 = f32[16,12,128]{2,1,0:T(8,128)S(1)} all-to-all(f32[16,12,128]{2,1,0:T(8,128)S(1)} %broadcast_in_dim.34), channel_id=1, replica_groups=mesh['grp'=4,'dp'=2,'yl'=2,'x'=4,'c'=2] {'grp','dp','yl'}, dimensions={0} | all-to-all | bytes 196608 | tf_op jit(solution)/shard_map/all_to_all | solution.py:176
  111.2 3.1 %fusion.55 = f32[512,1024]{1,0:T(8,128)S(1)} fusion(bf16[1024,1024]{1,0:T(8,128)(2,1)} %bitcast.149, f32[512,1024]{1,0:T(8,128)S(1)} %get-tuple-element.36, f32[512]{0:T(512)S(1)} %fusion.50, s32[1024]{0:T(1024)S(1)} %fusion.39, s32[512]{0:T(512)S(1)} %fusion.49, pred[]{:T(512)S(6)} %not.3), kind=kOutput, calls=%fused_computation.121 | convolution fusion | flops 1077936128 | bytes 6299649 | tf_op jit(solution)/shard_map/dot_general | solution.py:192
  119.7 12.3 %collective-permute-done.20 = f16[128,1024]{1,0:T(8,128)(2,1)S(1)} collective-permute-done((f16[128,1024]{1,0:T(8,128)(2,1)S(1)}, f16[128,1024]{1,0:T(8,128)(2,1)S(1)}, u32[]{:S(2)}, u32[]{:S(2)}) %collective-permute-start.20) | collective-permute-done | bytes 262176 | tf_op jit(solution)/shard_map/ppermute | solution.py:22
  133.6 4.0 %collective-permute-start.23 = (f16[128,1024]{1,0:T(8,128)(2,1)S(1)}, f16[128,1024]{1,0:T(8,128)(2,1)S(1)}, u32[]{:S(2)}, u32[]{:S(2)}) collective-permute-start(f16[128,1024]{1,0:T(8,128)(2,1)S(1)} %add_convert_fusion), channel_id=1, source_target_pairs={{0,96},{1,97},{2,98},{3,99},{4,100},{5,101},{6,102},{7,103},{8,104... | collective-permute-start | bytes 786440 | tf_op jit(solution)/shard_map/ppermute | solution.py:26
  139.4 4.7 %collective-permute-start.29 = (f16[128,1024]{1,0:T(8,128)(2,1)S(1)}, f16[128,1024]{1,0:T(8,128)(2,1)S(1)}, u32[]{:S(2)}, u32[]{:S(2)}) collective-permute-start(f16[128,1024]{1,0:T(8,128)(2,1)S(1)} %get-tuple-element.24), channel_id=1, source_target_pairs={{0,6},{2,0},{4,2},{6,4},{1,7},{3,1},{5,3},{7,5},{8,14},{10,8},{12,... | collective-permute-start | bytes 786440 | tf_op jit(solution)/shard_map/ppermute | solution.py:22
  147.0 3.3 %collective-permute-done.27 = f16[128,1024]{1,0:T(8,128)(2,1)S(1)} collective-permute-done((f16[128,1024]{1,0:T(8,128)(2,1)S(1)}, f16[128,1024]{1,0:T(8,128)(2,1)S(1)}, u32[]{:S(2)}, u32[]{:S(2)}) %collective-permute-start.27) | collective-permute-done | bytes 262176 | tf_op jit(solution)/shard_map/ppermute | solution.py:22
  150.3 4.0 %collective-permute-done.29 = f16[128,1024]{1,0:T(8,128)(2,1)S(1)} collective-permute-done((f16[128,1024]{1,0:T(8,128)(2,1)S(1)}, f16[128,1024]{1,0:T(8,128)(2,1)S(1)}, u32[]{:S(2)}, u32[]{:S(2)}) %collective-permute-start.29) | collective-permute-done | bytes 262176 | tf_op jit(solution)/shard_map/ppermute | solution.py:22
  156.9 3.8 %collective-permute-start.38 = (bf16[128,512]{1,0:T(8,128)(2,1)S(1)}, bf16[128,512]{1,0:T(8,128)(2,1)S(1)}, u32[]{:S(2)}, u32[]{:S(2)}) collective-permute-start(bf16[128,512]{1,0:T(8,128)(2,1)S(1)} %get-tuple-element.33), channel_id=1, source_target_pairs={{0,6},{2,0},{4,2},{6,4},{1,7},{3,1},{5,3},{7,5},{8,14},{10,8},{12,... | collective-permute-start | bytes 393224 | tf_op jit(solution)/shard_map/ppermute | solution.py:22
  169.1 12.0 %collective-permute-done.30 = bf16[128,512]{1,0:T(8,128)(2,1)S(1)} collective-permute-done((bf16[128,512]{1,0:T(8,128)(2,1)S(1)}, bf16[128,512]{1,0:T(8,128)(2,1)S(1)}, u32[]{:S(2)}, u32[]{:S(2)}) %collective-permute-start.30) | collective-permute-done | bytes 131104 | tf_op jit(solution)/shard_map/ppermute | solution.py:22
  184.8 12.0 %collective-permute-done.33.refs_3_ = bf16[2,128,512]{2,1,0:T(8,128)(2,1)S(1)} collective-permute-done((bf16[2,128,512]{2,1,0:T(8,128)(2,1)S(1)}, bf16[2,128,512]{2,1,0:T(8,128)(2,1)S(1)}, u32[]{:S(2)}, u32[]{:S(2)}) %collective-permute-start.33) | collective-permute-done | bytes 262176 | tf_op jit(solution)/shard_map/ppermute | solution.py:22
  201.9 21.7 %all_to_all.21.share = f32[8,32,1024]{2,1,0:T(8,128)S(1)} all-to-all(f32[8,32,1024]{2,1,0:T(8,128)S(1)} %bitcast.153), channel_id=1, replica_groups=mesh['grp'=4,'dp'=2,'yl'=2,'x'=4,'c'=2] {'grp','dp'}, dimensions={0} | all-to-all | bytes 2097152 | tf_op jit(solution)/shard_map/all_to_all | solution.py:232
  224.6 3.6 %all-to-all-start.3 = ((bf16[8,2,32,1024]{3,2,1,0:T(8,128)(2,1)}), bf16[8,2,32,1024]{3,2,1,0:T(8,128)(2,1)S(1)}, u32[]{:S(2)}, u32[]{:S(2)}) async-start(bf16[8,2,32,1024]{3,2,1,0:T(8,128)(2,1)} %shard_map.76), calls=%async_computation.3 | async-start | bytes 2097152 | tf_op jit(solution)/shard_map/all_to_all | solution.py:235
  234.8 3.3 %collective-permute-done.19 = f32[8,128]{1,0:T(8,128)S(1)} collective-permute-done((f32[8,128]{1,0:T(8,128)S(1)}, f32[8,128]{1,0:T(8,128)S(1)}, u32[]{:S(2)}, u32[]{:S(2)}) %collective-permute-start.19) | collective-permute-done | bytes 4128 | tf_op jit(solution)/shard_map/ppermute | solution.py:22
  240.2 4.5 %fusion = bf16[1,2048,256]{2,1,0:T(8,128)(2,1)} fusion(bf16[2048,1024]{1,0:T(8,128)(2,1)} %copy-done.1, bf16[256,1024]{1,0:T(8,128)(2,1)S(1)} %broadcast_select_fusion), kind=kOutput, calls=%fused_computation.3 | convolution fusion | flops 1074266112 | bytes 5767168 | tf_op jit(solution)/shard_map/dot_general | solution.py:228
  (149 shorter events, 73.1 us)
Async XLA Ops:
  0.7 19.9 %all-to-all-start = ((bf16[4,512,256]{2,1,0:T(8,128)(2,1)}), bf16[4,512,256]{2,1,0:T(8,128)(2,1)S(1)}, u32[]{:S(2)}, u32[]{:S(2)}) async-start(bf16[4,512,256]{2,1,0:T(8,128)(2,1)} %bitcast.150), calls=%async_computation | async-start | bytes 2097152 | tf_op jit(solution)/shard_map/all_to_all | solution.py:132
  4.4 16.1 %collective-permute-start.1 = (bf16[256,1024]{1,0:T(8,128)(2,1)S(1)}, bf16[256,1024]{1,0:T(8,128)(2,1)S(1)}, u32[]{:S(2)}, u32[]{:S(2)}) collective-permute-start(bf16[256,1024]{1,0:T(8,128)(2,1)S(1)} %broadcast_select_fusion), channel_id=1, source_target_pairs={{0,24},{8,16},{16,8},{24,0},{1,25},{9,17},{17,9},{25,1},{2,26},{10... | collective-permute-start | bytes 1572872 | tf_op jit(solution)/shard_map/ppermute | solution.py:129
  8.3 13.1 %collective-permute-start = (bf16[256,1024]{1,0:T(8,128)(2,1)S(1)}, bf16[256,1024]{1,0:T(8,128)(2,1)S(1)}, u32[]{:S(2)}, u32[]{:S(2)}) collective-permute-start(bf16[256,1024]{1,0:T(8,128)(2,1)S(1)} %broadcast_select_fusion), channel_id=1, source_target_pairs={{0,1},{1,0},{2,3},{3,2},{4,5},{5,4},{6,7},{7,6},{8,9},{9,8},{10,11... | collective-permute-start | bytes 1572872 | tf_op jit(solution)/shard_map/ppermute | solution.py:22
  25.4 16.6 %collective-permute-start.4 = (f32[128,1024]{1,0:T(8,128)}, f32[128,1024]{1,0:T(8,128)S(1)}, u32[]{:S(2)}, u32[]{:S(2)}) collective-permute-start(f32[128,1024]{1,0:T(8,128)} %get-tuple-element.26), channel_id=1, source_target_pairs={{0,4},{2,6},{4,0},{6,2},{1,5},{3,7},{5,1},{7,3},{8,12},{10,14},{12... | collective-permute-start | bytes 1572872 | tf_op jit(solution)/shard_map/ppermute | solution.py:22
  28.4 24.0 %collective-permute-start.5 = (f32[128,1024]{1,0:T(8,128)}, f32[128,1024]{1,0:T(8,128)}, u32[]{:S(2)}, u32[]{:S(2)}) collective-permute-start(f32[128,1024]{1,0:T(8,128)} %get-tuple-element.27), channel_id=1, source_target_pairs={{0,2},{2,4},{4,6},{6,0},{1,3},{3,5},{5,7},{7,1},{8,10},{10,12},{12... | collective-permute-start | bytes 1572872 | tf_op jit(solution)/shard_map/ppermute | solution.py:22
  29.0 23.5 %collective-permute-start.3 = (f32[128,1024]{1,0:T(8,128)}, f32[128,1024]{1,0:T(8,128)}, u32[]{:S(2)}, u32[]{:S(2)}) collective-permute-start(f32[128,1024]{1,0:T(8,128)} %get-tuple-element.28), channel_id=1, source_target_pairs={{0,6},{2,0},{4,2},{6,4},{1,7},{3,1},{5,3},{7,5},{8,14},{10,8},{12,... | collective-permute-start | bytes 1572872 | tf_op jit(solution)/shard_map/ppermute | solution.py:22
  54.2 14.1 %collective-permute-start.12 = (bf16[128,1024]{1,0:T(8,128)(2,1)S(1)}, bf16[128,1024]{1,0:T(8,128)(2,1)S(1)}, u32[]{:S(2)}, u32[]{:S(2)}) collective-permute-start(bf16[128,1024]{1,0:T(8,128)(2,1)S(1)} %fusion.51), channel_id=1, source_target_pairs={{0,6},{2,0},{4,2},{6,4},{1,7},{3,1},{5,3},{7,5},{8,14},{10,8},{12,... | collective-permute-start | bytes 786440 | tf_op jit(solution)/shard_map/ppermute | solution.py:22
  56.9 14.8 %collective-permute-start.14 = (bf16[128,1024]{1,0:T(8,128)(2,1)S(1)}, bf16[128,1024]{1,0:T(8,128)(2,1)S(1)}, u32[]{:S(2)}, u32[]{:S(2)}) collective-permute-start(bf16[128,1024]{1,0:T(8,128)(2,1)S(1)} %fusion.51), channel_id=1, source_target_pairs={{0,2},{2,4},{4,6},{6,0},{1,3},{3,5},{5,7},{7,1},{8,10},{10,12},{12... | collective-permute-start | bytes 786440 | tf_op jit(solution)/shard_map/ppermute | solution.py:22
  56.9 14.8 %collective-permute-start.13 = (bf16[128,1024]{1,0:T(8,128)(2,1)S(1)}, bf16[128,1024]{1,0:T(8,128)(2,1)S(1)}, u32[]{:S(2)}, u32[]{:S(2)}) collective-permute-start(bf16[128,1024]{1,0:T(8,128)(2,1)S(1)} %fusion.51), channel_id=1, source_target_pairs={{0,4},{2,6},{4,0},{6,2},{1,5},{3,7},{5,1},{7,3},{8,12},{10,14},{12... | collective-permute-start | bytes 786440 | tf_op jit(solution)/shard_map/ppermute | solution.py:22
  58.4 13.6 %collective-permute-start.8 = (bf16[128,1024]{1,0:T(8,128)(2,1)S(1)}, bf16[128,1024]{1,0:T(8,128)(2,1)}, u32[]{:S(2)}, u32[]{:S(2)}) collective-permute-start(bf16[128,1024]{1,0:T(8,128)(2,1)S(1)} %fusion.51), channel_id=1, source_target_pairs={{96,64},{97,65},{98,66},{99,67},{100,68},{101,69},{102,70},{103,71... | collective-permute-start | bytes 786440 | tf_op jit(solution)/shard_map/ppermute | solution.py:26
  71.8 20.4 %collective-permute-start.15 = (bf16[4,128,1024]{2,1,0:T(8,128)(2,1)S(1)}, bf16[4,128,1024]{2,1,0:T(8,128)(2,1)}, u32[]{:S(2)}, u32[]{:S(2)}) collective-permute-start(bf16[4,128,1024]{2,1,0:T(8,128)(2,1)S(1)} %get-tuple-element.30), channel_id=1, source_target_pairs={{0,1},{1,0},{2,3},{3,2},{4,5},{5,4},{6,7},{7,6},{8,9},{9,8},{10,11... | collective-permute-start | bytes 3145736 | tf_op jit(solution)/shard_map/ppermute | solution.py:22
  116.2 21.4 %collective-permute-start.26 = (f32[4,128,1024]{2,1,0:T(8,128)S(1)}, f32[4,128,1024]{2,1,0:T(8,128)S(1)}, u32[]{:S(2)}, u32[]{:S(2)}) collective-permute-start(f32[4,128,1024]{2,1,0:T(8,128)S(1)} %slice_bitcast_fusion), channel_id=1, source_target_pairs={{0,1},{1,0},{2,3},{3,2},{4,5},{5,4},{6,7},{7,6},{8,9},{9,8},{10,11... | collective-permute-start | bytes 6291464 | tf_op jit(solution)/shard_map/ppermute | solution.py:22
  116.4 15.6 %collective-permute-start.20 = (f16[128,1024]{1,0:T(8,128)(2,1)S(1)}, f16[128,1024]{1,0:T(8,128)(2,1)S(1)}, u32[]{:S(2)}, u32[]{:S(2)}) collective-permute-start(f16[128,1024]{1,0:T(8,128)(2,1)S(1)} %get-tuple-element.20), channel_id=1, source_target_pairs={{0,8},{8,16},{16,24},{24,0},{1,9},{9,17},{17,25},{25,1},{2,10},{10... | collective-permute-start | bytes 786440 | tf_op jit(solution)/shard_map/ppermute | solution.py:22
  117.0 15.0 %collective-permute-start.22 = (f16[128,1024]{1,0:T(8,128)(2,1)S(1)}, f16[128,1024]{1,0:T(8,128)(2,1)S(1)}, u32[]{:S(2)}, u32[]{:S(2)}) collective-permute-start(f16[128,1024]{1,0:T(8,128)(2,1)S(1)} %get-tuple-element.21), channel_id=1, source_target_pairs={{0,24},{8,0},{16,8},{24,16},{1,25},{9,1},{17,9},{25,17},{2,26},{10... | collective-permute-start | bytes 786440 | tf_op jit(solution)/shard_map/ppermute | solution.py:22
  133.6 13.5 %collective-permute-start.23 = (f16[128,1024]{1,0:T(8,128)(2,1)S(1)}, f16[128,1024]{1,0:T(8,128)(2,1)S(1)}, u32[]{:S(2)}, u32[]{:S(2)}) collective-permute-start(f16[128,1024]{1,0:T(8,128)(2,1)S(1)} %add_convert_fusion), channel_id=1, source_target_pairs={{0,96},{1,97},{2,98},{3,99},{4,100},{5,101},{6,102},{7,103},{8,104... | collective-permute-start | bytes 786440 | tf_op jit(solution)/shard_map/ppermute | solution.py:26
  139.4 14.9 %collective-permute-start.29 = (f16[128,1024]{1,0:T(8,128)(2,1)S(1)}, f16[128,1024]{1,0:T(8,128)(2,1)S(1)}, u32[]{:S(2)}, u32[]{:S(2)}) collective-permute-start(f16[128,1024]{1,0:T(8,128)(2,1)S(1)} %get-tuple-element.24), channel_id=1, source_target_pairs={{0,6},{2,0},{4,2},{6,4},{1,7},{3,1},{5,3},{7,5},{8,14},{10,8},{12,... | collective-permute-start | bytes 786440 | tf_op jit(solution)/shard_map/ppermute | solution.py:22
  167.0 17.7 %collective-permute-start.41 = (bf16[4,128,512]{2,1,0:T(8,128)(2,1)S(1)}, bf16[4,128,512]{2,1,0:T(8,128)(2,1)S(1)}, u32[]{:S(2)}, u32[]{:S(2)}) collective-permute-start(bf16[4,128,512]{2,1,0:T(8,128)(2,1)S(1)} %pad_maximum_fusion.3.refs_8_), channel_id=1, source_target_pairs={{0,8},{8,0},{1,9},{9,1},{2,10},{10,2},{3,11},{11,3},{4,12},{12,4},... | collective-permute-start | bytes 1572872 | tf_op jit(solution)/shard_map/ppermute | solution.py:22
  168.3 12.8 %collective-permute-start.30 = (bf16[128,512]{1,0:T(8,128)(2,1)S(1)}, bf16[128,512]{1,0:T(8,128)(2,1)S(1)}, u32[]{:S(2)}, u32[]{:S(2)}) collective-permute-start(bf16[128,512]{1,0:T(8,128)(2,1)S(1)} %get-tuple-element.34), channel_id=1, source_target_pairs={{0,8},{8,0},{1,9},{9,1},{2,10},{10,2},{3,11},{11,3},{4,12},{12,4},... | collective-permute-start | bytes 393224 | tf_op jit(solution)/shard_map/ppermute | solution.py:22
  181.2 15.5 %collective-permute-start.33 = (bf16[2,128,512]{2,1,0:T(8,128)(2,1)S(1)}, bf16[2,128,512]{2,1,0:T(8,128)(2,1)S(1)}, u32[]{:S(2)}, u32[]{:S(2)}) collective-permute-start(bf16[2,128,512]{2,1,0:T(8,128)(2,1)S(1)} %pad_maximum_fusion.4.refs_0_), channel_id=1, source_target_pairs={{0,2},{2,4},{4,6},{6,0},{1,3},{3,5},{5,7},{7,1},{8,10},{10,12},{12... | collective-permute-start | bytes 786440 | tf_op jit(solution)/shard_map/ppermute | solution.py:22
  181.3 15.5 %collective-permute-start.32 = (bf16[2,128,512]{2,1,0:T(8,128)(2,1)S(1)}, bf16[2,128,512]{2,1,0:T(8,128)(2,1)S(1)}, u32[]{:S(2)}, u32[]{:S(2)}) collective-permute-start(bf16[2,128,512]{2,1,0:T(8,128)(2,1)S(1)} %pad_maximum_fusion.4.refs_0_), channel_id=1, source_target_pairs={{0,4},{2,6},{4,0},{6,2},{1,5},{3,7},{5,1},{7,3},{8,12},{10,14},{12... | collective-permute-start | bytes 786440 | tf_op jit(solution)/shard_map/ppermute | solution.py:22
  182.6 15.1 %collective-permute-start.42 = (bf16[4,128,512]{2,1,0:T(8,128)(2,1)S(1)}, bf16[4,128,512]{2,1,0:T(8,128)(2,1)S(1)}, u32[]{:S(2)}, u32[]{:S(2)}) collective-permute-start(bf16[4,128,512]{2,1,0:T(8,128)(2,1)S(1)} %pad_maximum_fusion.3.refs_8_), channel_id=1, source_target_pairs={{0,1},{1,0},{2,3},{3,2},{4,5},{5,4},{6,7},{7,6},{8,9},{9,8},{10,11... | collective-permute-start | bytes 1572872 | tf_op jit(solution)/shard_map/ppermute | solution.py:22
  182.7 14.6 %collective-permute-start.31 = (bf16[2,128,512]{2,1,0:T(8,128)(2,1)S(1)}, bf16[2,128,512]{2,1,0:T(8,128)(2,1)S(1)}, u32[]{:S(2)}, u32[]{:S(2)}) collective-permute-start(bf16[2,128,512]{2,1,0:T(8,128)(2,1)S(1)} %pad_maximum_fusion.4.refs_0_), channel_id=1, source_target_pairs={{0,6},{2,0},{4,2},{6,4},{1,7},{3,1},{5,3},{7,5},{8,14},{10,8},{12,... | collective-permute-start | bytes 786440 | tf_op jit(solution)/shard_map/ppermute | solution.py:22
  184.7 14.4 %collective-permute-start.43 = (bf16[4,128,512]{2,1,0:T(8,128)(2,1)S(1)}, bf16[4,128,512]{2,1,0:T(8,128)(2,1)S(1)}, u32[]{:S(2)}, u32[]{:S(2)}) collective-permute-start(bf16[4,128,512]{2,1,0:T(8,128)(2,1)S(1)} %collective-permute-done.41.refs_9_), channel_id=1, source_target_pairs={{0,1},{1,0},{2,3},{3,2},{4,5},{5,4},{6,7},{7,6},{8,9},{9,8},{10,11... | collective-permute-start | bytes 1572872 | tf_op jit(solution)/shard_map/ppermute | solution.py:22
  224.6 20.1 %all-to-all-start.3 = ((bf16[8,2,32,1024]{3,2,1,0:T(8,128)(2,1)}), bf16[8,2,32,1024]{3,2,1,0:T(8,128)(2,1)S(1)}, u32[]{:S(2)}, u32[]{:S(2)}) async-start(bf16[8,2,32,1024]{3,2,1,0:T(8,128)(2,1)} %shard_map.76), calls=%async_computation.3 | async-start | bytes 2097152 | tf_op jit(solution)/shard_map/all_to_all | solution.py:235
  (32 other events, 214.4 us)

commit v2 on v1

--- a/solution.py
+++ b/solution.py
@@ -29,11 +29,6 @@
 def turned(array, shift):
     n = array.shape[0]
     return lax.dynamic_slice_in_dim(jnp.concatenate([array, array]), shift, n, 0)
-
-
-def part(array, index, count):
-    size = array.shape[0] // count
-    return lax.dynamic_slice_in_dim(array, index * size, size, 0)
 
 
 def row_order_kernel(at, *refs):
@@ -129,7 +124,8 @@
     outer = lax.ppermute(weight, Y, [(k, 3 - k) for k in range(4)])
     other = fetch(weight, "c", 1)
     outer_other = fetch(outer, "c", 1)
-    mine = lax.all_to_all(features.reshape(4, rows // 4, feats), ("yl", "c"), 0, 0, tiled=True)
+    mine = features.reshape(4, rows // 4, feats)
+    mine = lax.all_to_all(mine, ("yl", "c"), 0, 0, tiled=True)
     sources = ((2 * yl + c, weight), (2 * yl + 1 - c, other))
     sources += ((2 - 2 * yl + c, outer), (3 - 2 * yl - c, outer_other))
     partial = sum(
@@ -140,22 +136,33 @@
         )
         for k, w in sources
     )
-    summed = part(partial, x, 4) + sum(
-        fetch(part(partial, (x - k) % 4, 4), "x", k) for k in (1, 2, 3)
-    )
-    row_norms = jnp.sqrt(jnp.sum(summed * summed, axis=-1, keepdims=True) + epsilon_norm)
-    unit_rows = summed / row_norms
-    embedded = unit_rows.astype(jnp.bfloat16)
-
-    sent = [one_way(embedded, "grp", 3, k) for k in range(3)]
+    halves = partial.reshape(4, 2, per // 2, emb)
+
+    def piece(k, h):
+        return lax.dynamic_index_in_dim(halves[:, h], (x - k) % 4, 0, keepdims=False)
+
+    units, norms, embeds = [], [], []
+    for h in (0, 1):
+        arrived = [fetch(piece(k, h), "x", k) for k in (1, 2, 3)]
+        summed = piece(0, h) + sum(arrived)
+        row_norms = jnp.sqrt(jnp.sum(summed * summed, axis=-1, keepdims=True) + epsilon_norm)
+        units.append(summed / row_norms)
+        norms.append(row_norms)
+        embeds.append(units[h].astype(jnp.bfloat16))
+
+    sent = []
+    for h in (0, 1):
+        sent.append([one_way(embeds[h], "grp", 3, k) for k in range(3)])
+    sent = [jnp.concatenate(both) for both in zip(*sent)]
+    embedded = lax.optimization_barrier(jnp.concatenate(embeds))
+    query = jnp.where(
+        is_query, embedded, jnp.where(z == 0, sent[0], jnp.where(z == 1, sent[1], sent[2]))
+    )
+    around = [fetch(query, Y, k) for k in (1, 2, 3)]
+    queries = jnp.stack([query] + around).reshape(4 * per, emb)
     passages = jnp.stack([embedded] + [fetch(embedded, "x", k) for k in (1, 2, 3)])
     swapped = fetch(passages, "c", 1)
-    passages = jnp.stack([passages, swapped], axis=1).reshape(8 * per, emb)
-    query = jnp.where(
-        is_query, embedded, jnp.where(z == 0, sent[0], jnp.where(z == 1, sent[1], sent[2]))
-    )
-    around = [fetch(query, Y, k) for k in (1, 2, 3)]
-    queries = jnp.stack([query] + around).reshape(4 * per, emb)
+    passages = jnp.stack([passages, swapped]).reshape(8 * per, emb)
 
     logits = inverse_temp * lax.dot_general(
         queries, passages, (((1,), (1,)), ((), ())), preferred_element_type=jnp.float32
@@ -165,7 +172,7 @@
     ids = turned(ids, y).reshape(4 * per)
     k = lax.broadcasted_iota(jnp.int32, (8, per), 0)
     i = lax.broadcasted_iota(jnp.int32, (8, per), 1)
-    owner = (yl * 2 + (c + k) % 2) * 4 + (x + k // 2) % 4
+    owner = (yl * 2 + (c + k // 4) % 2) * 4 + (x + k) % 4
     column_ids = (z * total_q + yh * rows + owner * per + i).reshape(1, 8 * per)
     hit = ids[:, None] == column_ids
     positive_part = jnp.sum(jnp.where(hit, logits, 0.0), axis=1)
@@ -195,8 +202,8 @@
     )
     dquery, dpassage = lax.optimization_barrier((dquery, dpassage))
     dquery = dquery.reshape(4, per, emb)
-    dpassage = dpassage.reshape(4, 2, per, emb)
-    dpassage = dpassage[:, 0] + fetch(dpassage[:, 1], "c", 1)
+    dpassage = dpassage.reshape(2, 4, per, emb)
+    dpassage = dpassage[0] + fetch(dpassage[1], "c", 1)
     dq_parts = [
         fetch((dquery[k] * dq_unit).astype(jnp.float16), Y, 4 - k).astype(jnp.float32)
         for k in (1, 2, 3)
@@ -211,8 +218,11 @@
     dquery = sum(one_way(half, "grp", k, 3).astype(jnp.float32) for k in range(3))
 
     grad_emb = inverse_temp * jnp.where(is_query, dquery / dq_unit, dpassage / dp_unit)
-    inner = jnp.sum(unit_rows * grad_emb, axis=-1, keepdims=True)
-    grad_proj = ((grad_emb - unit_rows * inner) / row_norms).astype(jnp.bfloat16)
+    grad_halves = []
+    for unit_rows, row_norms, g in zip(units, norms, jnp.split(grad_emb, 2)):
+        inner = jnp.sum(unit_rows * g, axis=-1, keepdims=True)
+        grad_halves.append(((g - unit_rows * inner) / row_norms).astype(jnp.bfloat16))
+    grad_proj = jnp.concatenate(grad_halves)
 
     left, right = grad_proj[:, : emb // 2], grad_proj[:, emb // 2 :]
     left = jnp.stack([left, fetch(left, "yl", 1)])

time: 249 us -> 254 us (1.020)
  starting transfers between devices: 60.5 us -> 63.7 us
  other arithmetic: 11 us -> 14 us
  blocking collectives: 35.5 us -> 32.9 us
    ppermute x6 -> x9, waiting for transfers between devices: 7.57 us -> 14.7 us  [one_way(): return lax.ppermute(array, axis, [(source, target)])]
    ppermute x37 -> x40, waiting for transfers between devices: 95.7 us -> 91.4 us  [fetch(): lax.ppermute(array, axis, [(k, (k - step) % size) for k in range(size)])]
    all_to_all x1, blocking collectives: 13.8 us -> 11.2 us  [local(): lax.all_to_all(jnp.broadcast_to(stats.reshape(1, 12, per), (16, 12, per))...]
    ppermute x6 -> x9, starting transfers between devices: 9.36 us -> 11.9 us  [one_way(): return lax.ppermute(array, axis, [(source, target)])]
    ppermute x37 -> x40, starting transfers between devices: 40 us -> 40.7 us  [fetch(): lax.ppermute(array, axis, [(k, (k - step) % size) for k in range(size)])]
  transfers between devices with their start and end apart: 46 -> 52, of which waited for: 28 -> 31; matrix products, arithmetic and copies ran while one was open for 5% -> 7% of each run, Pallas kernels for 0% -> 0%
where the time goes in v2:
time: 254 us; the launch traced here: 253 us
  waiting for transfers between devices  118 us (46%)
  starting transfers between devices  63.7 us (25%)
  blocking collectives  32.9 us (13%)
  other arithmetic  14 us (6%)
  matrix products  13.6 us (5%)
  local copies, waits for them, and re-layouts  3.57 us (1%)
  Pallas kernels  3.33 us (1%)
  between operations  3.05 us (1%)
    ppermute x40, waiting for transfers between devices, fetch(): lax.ppermute(array, axis, [(k, (k - step) % size) for k in range(size)])  91.4 us
    ppermute x40, starting transfers between devices, fetch(): lax.ppermute(array, axis, [(k, (k - step) % size) for k in range(size)])  40.7 us
    all_to_all x1, blocking collectives, local(): lax.all_to_all(weight_part.reshape(8, feats // 8, emb), ('grp', 'dp'), 0,...  21.7 us
    ppermute x9, waiting for transfers between devices, one_way(): return lax.ppermute(array, axis, [(source, target)])  14.7 us
    ppermute x1, waiting for transfers between devices, local(): outer = lax.ppermute(weight, Y, [(k, 3 - k) for k in range(4)])  12.2 us
    ppermute x9, starting transfers between devices, one_way(): return lax.ppermute(array, axis, [(source, target)])  11.9 us
    all_to_all x1, blocking collectives, local(): lax.all_to_all(jnp.broadcast_to(stats.reshape(1, 12, per), (16, 12, per))...  11.2 us
  transfers between devices with their start and end apart: 52, of which 31 were waited for; matrix products, arithmetic and copies ran while one was open for 7% of the time, Pallas kernels for 0%

profile of v2, /device:TPU:0, one launch (start us, length us, event | category | flops | bytes accessed | tf_op | source)
XLA Modules:
  0.0 252.6 jit_solution(16176620740714457085)
XLA Ops:
  0.7 3.7 %all-to-all-start = ((bf16[4,512,256]{2,1,0:T(8,128)(2,1)}), bf16[4,512,256]{2,1,0:T(8,128)(2,1)S(1)}, u32[]{:S(2)}, u32[]{:S(2)}) async-start(bf16[4,512,256]{2,1,0:T(8,128)(2,1)} %bitcast.134), calls=%async_computation | async-start | bytes 2097152 | tf_op jit(solution)/shard_map/all_to_all | solution.py:128
  4.4 3.9 %collective-permute-start.1 = (bf16[256,1024]{1,0:T(8,128)(2,1)S(1)}, bf16[256,1024]{1,0:T(8,128)(2,1)S(1)}, u32[]{:S(2)}, u32[]{:S(2)}) collective-permute-start(bf16[256,1024]{1,0:T(8,128)(2,1)S(1)} %broadcast_select_fusion), channel_id=1, source_target_pairs={{0,24},{8,16},{16,8},{24,0},{1,25},{9,17},{17,9},{25,1},{2,26},{10... | collective-permute-start | bytes 1572872 | tf_op jit(solution)/shard_map/ppermute | solution.py:124
  8.3 12.2 %collective-permute-done.1 = bf16[256,1024]{1,0:T(8,128)(2,1)S(1)} collective-permute-done((bf16[256,1024]{1,0:T(8,128)(2,1)S(1)}, bf16[256,1024]{1,0:T(8,128)(2,1)S(1)}, u32[]{:S(2)}, u32[]{:S(2)}) %collective-permute-start.1) | collective-permute-done | bytes 524320 | tf_op jit(solution)/shard_map/ppermute | solution.py:124
  30.5 3.6 %collective-permute-done.4 = f32[64,1024]{1,0:T(8,128)} collective-permute-done((f32[64,1024]{1,0:T(8,128)S(1)}, f32[64,1024]{1,0:T(8,128)}, u32[]{:S(2)}, u32[]{:S(2)}) %collective-permute-start.4) | collective-permute-done | bytes 262176 | tf_op jit(solution)/shard_map/ppermute | solution.py:22
  41.0 4.2 %collective-permute-done.7 = f32[64,1024]{1,0:T(8,128)S(1)} collective-permute-done((f32[64,1024]{1,0:T(8,128)S(1)}, f32[64,1024]{1,0:T(8,128)S(1)}, u32[]{:S(2)}, u32[]{:S(2)}) %collective-permute-start.7) | collective-permute-done | bytes 262176 | tf_op jit(solution)/shard_map/ppermute | solution.py:22
  45.2 4.7 %collective-permute-done.8 = f32[64,1024]{1,0:T(8,128)S(1)} collective-permute-done((f32[64,1024]{1,0:T(8,128)S(1)}, f32[64,1024]{1,0:T(8,128)S(1)}, u32[]{:S(2)}, u32[]{:S(2)}) %collective-permute-start.8) | collective-permute-done | bytes 262176 | tf_op jit(solution)/shard_map/ppermute | solution.py:22
  58.1 3.2 %collective-permute-done.20 = bf16[128,1024]{1,0:T(8,128)(2,1)S(1)} collective-permute-done((bf16[128,1024]{1,0:T(8,128)(2,1)S(1)}, bf16[128,1024]{1,0:T(8,128)(2,1)S(1)}, u32[]{:S(2)}, u32[]{:S(2)}) %collective-permute-start.20) | collective-permute-done | bytes 262176 | tf_op jit(solution)/shard_map/ppermute | solution.py:22
  61.4 6.6 %collective-permute-done.19 = bf16[128,1024]{1,0:T(8,128)(2,1)S(1)} collective-permute-done((bf16[128,1024]{1,0:T(8,128)(2,1)S(1)}, bf16[128,1024]{1,0:T(8,128)(2,1)S(1)}, u32[]{:S(2)}, u32[]{:S(2)}) %collective-permute-start.19) | collective-permute-done | bytes 262176 | tf_op jit(solution)/shard_map/ppermute | solution.py:22
  75.0 3.9 %collective-permute-done.9 = bf16[64,1024]{1,0:T(8,128)(2,1)} collective-permute-done((bf16[64,1024]{1,0:T(8,128)(2,1)}, bf16[64,1024]{1,0:T(8,128)(2,1)}, u32[]{:S(2)}, u32[]{:S(2)}) %collective-permute-start.9) | collective-permute-done | bytes 131104 | tf_op jit(solution)/shard_map/ppermute | solution.py:26
  78.9 5.7 %collective-permute-done.10 = bf16[64,1024]{1,0:T(8,128)(2,1)} collective-permute-done((bf16[64,1024]{1,0:T(8,128)(2,1)S(1)}, bf16[64,1024]{1,0:T(8,128)(2,1)}, u32[]{:S(2)}, u32[]{:S(2)}) %collective-permute-start.10) | collective-permute-done | bytes 131104 | tf_op jit(solution)/shard_map/ppermute | solution.py:26
  86.8 4.4 %collective-permute-start.16 = (bf16[128,1024]{1,0:T(8,128)(2,1)}, bf16[128,1024]{1,0:T(8,128)(2,1)}, u32[]{:S(2)}, u32[]{:S(2)}) collective-permute-start(bf16[128,1024]{1,0:T(8,128)(2,1)} %fusion.18), channel_id=1, source_target_pairs={{0,16},{8,24},{16,0},{24,8},{1,17},{9,25},{17,1},{25,9},{2,18},{10... | collective-permute-start | bytes 786440 | tf_op jit(solution)/shard_map/ppermute | solution.py:22
  91.9 4.2 %collective-permute-done.17 = bf16[128,1024]{1,0:T(8,128)(2,1)S(1)} collective-permute-done((bf16[128,1024]{1,0:T(8,128)(2,1)}, bf16[128,1024]{1,0:T(8,128)(2,1)S(1)}, u32[]{:S(2)}, u32[]{:S(2)}) %collective-permute-start.17) | collective-permute-done | bytes 262176 | tf_op jit(solution)/shard_map/ppermute | solution.py:22
  96.2 6.8 %collective-permute-done.16 = bf16[128,1024]{1,0:T(8,128)(2,1)} collective-permute-done((bf16[128,1024]{1,0:T(8,128)(2,1)}, bf16[128,1024]{1,0:T(8,128)(2,1)}, u32[]{:S(2)}, u32[]{:S(2)}) %collective-permute-start.16) | collective-permute-done | bytes 262176 | tf_op jit(solution)/shard_map/ppermute | solution.py:22
  107.5 11.2 %all_to_all.20 = f32[16,12,128]{2,1,0:T(8,128)S(1)} all-to-all(f32[16,12,128]{2,1,0:T(8,128)S(1)} %broadcast_in_dim.36), channel_id=1, replica_groups=mesh['grp'=4,'dp'=2,'yl'=2,'x'=4,'c'=2] {'grp','dp','yl'}, dimensions={0} | all-to-all | bytes 196608 | tf_op jit(solution)/shard_map/all_to_all | solution.py:183
  128.4 12.3 %collective-permute-done.26 = f16[128,1024]{1,0:T(8,128)(2,1)S(1)} collective-permute-done((f16[128,1024]{1,0:T(8,128)(2,1)S(1)}, f16[128,1024]{1,0:T(8,128)(2,1)S(1)}, u32[]{:S(2)}, u32[]{:S(2)}) %collective-permute-start.26) | collective-permute-done | bytes 262176 | tf_op jit(solution)/shard_map/ppermute | solution.py:22
  142.3 4.0 %collective-permute-start.29 = (f16[128,1024]{1,0:T(8,128)(2,1)S(1)}, f16[128,1024]{1,0:T(8,128)(2,1)S(1)}, u32[]{:S(2)}, u32[]{:S(2)}) collective-permute-start(f16[128,1024]{1,0:T(8,128)(2,1)S(1)} %add_convert_fusion), channel_id=1, source_target_pairs={{0,96},{1,97},{2,98},{3,99},{4,100},{5,101},{6,102},{7,103},{8,104... | collective-permute-start | bytes 786440 | tf_op jit(solution)/shard_map/ppermute | solution.py:26
  150.7 5.1 %collective-permute-done.29 = f16[128,1024]{1,0:T(8,128)(2,1)S(1)} collective-permute-done((f16[128,1024]{1,0:T(8,128)(2,1)S(1)}, f16[128,1024]{1,0:T(8,128)(2,1)S(1)}, u32[]{:S(2)}, u32[]{:S(2)}) %collective-permute-start.29) | collective-permute-done | bytes 262176 | tf_op jit(solution)/shard_map/ppermute | solution.py:26
  156.9 3.3 %collective-permute-done.35 = f16[128,1024]{1,0:T(8,128)(2,1)S(1)} collective-permute-done((f16[128,1024]{1,0:T(8,128)(2,1)S(1)}, f16[128,1024]{1,0:T(8,128)(2,1)S(1)}, u32[]{:S(2)}, u32[]{:S(2)}) %collective-permute-start.35) | collective-permute-done | bytes 262176 | tf_op jit(solution)/shard_map/ppermute | solution.py:22
  174.4 12.0 %collective-permute-done.36 = bf16[128,512]{1,0:T(8,128)(2,1)S(1)} collective-permute-done((bf16[128,512]{1,0:T(8,128)(2,1)S(1)}, bf16[128,512]{1,0:T(8,128)(2,1)S(1)}, u32[]{:S(2)}, u32[]{:S(2)}) %collective-permute-start.36) | collective-permute-done | bytes 131104 | tf_op jit(solution)/shard_map/ppermute | solution.py:22
  190.1 12.0 %collective-permute-done.39.refs_3_ = bf16[2,128,512]{2,1,0:T(8,128)(2,1)S(1)} collective-permute-done((bf16[2,128,512]{2,1,0:T(8,128)(2,1)S(1)}, bf16[2,128,512]{2,1,0:T(8,128)(2,1)S(1)}, u32[]{:S(2)}, u32[]{:S(2)}) %collective-permute-start.39) | collective-permute-done | bytes 262176 | tf_op jit(solution)/shard_map/ppermute | solution.py:22
  207.2 21.7 %all_to_all.21.share = f32[8,32,1024]{2,1,0:T(8,128)S(1)} all-to-all(f32[8,32,1024]{2,1,0:T(8,128)S(1)} %bitcast.137), channel_id=1, replica_groups=mesh['grp'=4,'dp'=2,'yl'=2,'x'=4,'c'=2] {'grp','dp'}, dimensions={0} | all-to-all | bytes 2097152 | tf_op jit(solution)/shard_map/all_to_all | solution.py:242
  230.0 3.6 %all-to-all-start.3 = ((bf16[8,2,32,1024]{3,2,1,0:T(8,128)(2,1)}), bf16[8,2,32,1024]{3,2,1,0:T(8,128)(2,1)S(1)}, u32[]{:S(2)}, u32[]{:S(2)}) async-start(bf16[8,2,32,1024]{3,2,1,0:T(8,128)(2,1)} %shard_map.76), calls=%async_computation.3 | async-start | bytes 2097152 | tf_op jit(solution)/shard_map/all_to_all | solution.py:245
  240.2 3.3 %collective-permute-done.25 = f32[8,128]{1,0:T(8,128)S(1)} collective-permute-done((f32[8,128]{1,0:T(8,128)S(1)}, f32[8,128]{1,0:T(8,128)S(1)}, u32[]{:S(2)}, u32[]{:S(2)}) %collective-permute-start.25) | collective-permute-done | bytes 4128 | tf_op jit(solution)/shard_map/ppermute | solution.py:22
  245.6 4.5 %fusion = bf16[1,2048,256]{2,1,0:T(8,128)(2,1)} fusion(bf16[2048,1024]{1,0:T(8,128)(2,1)} %copy-done.2, bf16[256,1024]{1,0:T(8,128)(2,1)S(1)} %broadcast_select_fusion), kind=kOutput, calls=%fused_computation.3 | convolution fusion | flops 1074266112 | bytes 5767168 | tf_op jit(solution)/shard_map/dot_general | solution.py:238
  (180 shorter events, 89.6 us)
Async XLA Ops:
  0.7 19.9 %all-to-all-start = ((bf16[4,512,256]{2,1,0:T(8,128)(2,1)}), bf16[4,512,256]{2,1,0:T(8,128)(2,1)S(1)}, u32[]{:S(2)}, u32[]{:S(2)}) async-start(bf16[4,512,256]{2,1,0:T(8,128)(2,1)} %bitcast.134), calls=%async_computation | async-start | bytes 2097152 | tf_op jit(solution)/shard_map/all_to_all | solution.py:128
  4.4 16.1 %collective-permute-start.1 = (bf16[256,1024]{1,0:T(8,128)(2,1)S(1)}, bf16[256,1024]{1,0:T(8,128)(2,1)S(1)}, u32[]{:S(2)}, u32[]{:S(2)}) collective-permute-start(bf16[256,1024]{1,0:T(8,128)(2,1)S(1)} %broadcast_select_fusion), channel_id=1, source_target_pairs={{0,24},{8,16},{16,8},{24,0},{1,25},{9,17},{17,9},{25,1},{2,26},{10... | collective-permute-start | bytes 1572872 | tf_op jit(solution)/shard_map/ppermute | solution.py:124
  8.3 13.1 %collective-permute-start = (bf16[256,1024]{1,0:T(8,128)(2,1)S(1)}, bf16[256,1024]{1,0:T(8,128)(2,1)S(1)}, u32[]{:S(2)}, u32[]{:S(2)}) collective-permute-start(bf16[256,1024]{1,0:T(8,128)(2,1)S(1)} %broadcast_select_fusion), channel_id=1, source_target_pairs={{0,1},{1,0},{2,3},{3,2},{4,5},{5,4},{6,7},{7,6},{8,9},{9,8},{10,11... | collective-permute-start | bytes 1572872 | tf_op jit(solution)/shard_map/ppermute | solution.py:22
  26.2 13.5 %collective-permute-start.5 = (f32[64,1024]{1,0:T(8,128)S(1)}, f32[64,1024]{1,0:T(8,128)}, u32[]{:S(2)}, u32[]{:S(2)}) collective-permute-start(f32[64,1024]{1,0:T(8,128)S(1)} %get-tuple-element.35), channel_id=1, source_target_pairs={{0,2},{2,4},{4,6},{6,0},{1,3},{3,5},{5,7},{7,1},{8,10},{10,12},{12... | collective-permute-start | bytes 786440 | tf_op jit(solution)/shard_map/ppermute | solution.py:22
  26.8 12.9 %collective-permute-start.3 = (f32[64,1024]{1,0:T(8,128)S(1)}, f32[64,1024]{1,0:T(8,128)}, u32[]{:S(2)}, u32[]{:S(2)}) collective-permute-start(f32[64,1024]{1,0:T(8,128)S(1)} %get-tuple-element.36), channel_id=1, source_target_pairs={{0,6},{2,0},{4,2},{6,4},{1,7},{3,1},{5,3},{7,5},{8,14},{10,8},{12,... | collective-permute-start | bytes 786440 | tf_op jit(solution)/shard_map/ppermute | solution.py:22
  29.5 15.7 %collective-permute-start.7 = (f32[64,1024]{1,0:T(8,128)S(1)}, f32[64,1024]{1,0:T(8,128)S(1)}, u32[]{:S(2)}, u32[]{:S(2)}) collective-permute-start(f32[64,1024]{1,0:T(8,128)S(1)} %get-tuple-element.37), channel_id=1, source_target_pairs={{0,4},{2,6},{4,0},{6,2},{1,5},{3,7},{5,1},{7,3},{8,12},{10,14},{12... | collective-permute-start | bytes 786440 | tf_op jit(solution)/shard_map/ppermute | solution.py:22
  29.6 20.3 %collective-permute-start.8 = (f32[64,1024]{1,0:T(8,128)S(1)}, f32[64,1024]{1,0:T(8,128)S(1)}, u32[]{:S(2)}, u32[]{:S(2)}) collective-permute-start(f32[64,1024]{1,0:T(8,128)S(1)} %get-tuple-element.38), channel_id=1, source_target_pairs={{0,2},{2,4},{4,6},{6,0},{1,3},{3,5},{5,7},{7,1},{8,10},{10,12},{12... | collective-permute-start | bytes 786440 | tf_op jit(solution)/shard_map/ppermute | solution.py:22
  34.1 16.0 %collective-permute-start.6 = (f32[64,1024]{1,0:T(8,128)S(1)}, f32[64,1024]{1,0:T(8,128)S(1)}, u32[]{:S(2)}, u32[]{:S(2)}) collective-permute-start(f32[64,1024]{1,0:T(8,128)S(1)} %get-tuple-element.39), channel_id=1, source_target_pairs={{0,6},{2,0},{4,2},{6,4},{1,7},{3,1},{5,3},{7,5},{8,14},{10,8},{12,... | collective-permute-start | bytes 786440 | tf_op jit(solution)/shard_map/ppermute | solution.py:22
  53.5 14.4 %collective-permute-start.19 = (bf16[128,1024]{1,0:T(8,128)(2,1)S(1)}, bf16[128,1024]{1,0:T(8,128)(2,1)S(1)}, u32[]{:S(2)}, u32[]{:S(2)}) collective-permute-start(bf16[128,1024]{1,0:T(8,128)(2,1)S(1)} %pad_maximum_fusion.4), channel_id=1, source_target_pairs={{0,4},{2,6},{4,0},{6,2},{1,5},{3,7},{5,1},{7,3},{8,12},{10,14},{12... | collective-permute-start | bytes 786440 | tf_op jit(solution)/shard_map/ppermute | solution.py:22
  56.8 15.0 %collective-permute-start.13 = (bf16[64,1024]{1,0:T(8,128)(2,1)}, bf16[64,1024]{1,0:T(8,128)(2,1)S(1)}, u32[]{:S(2)}, u32[]{:S(2)}) collective-permute-start(bf16[64,1024]{1,0:T(8,128)(2,1)} %fusion.49), channel_id=1, source_target_pairs={{96,64},{97,65},{98,66},{99,67},{100,68},{101,69},{102,70},{103,71... | collective-permute-start | bytes 393224 | tf_op jit(solution)/shard_map/ppermute | solution.py:26
  57.5 15.6 %collective-permute-start.11 = (bf16[64,1024]{1,0:T(8,128)(2,1)}, bf16[64,1024]{1,0:T(8,128)(2,1)S(1)}, u32[]{:S(2)}, u32[]{:S(2)}) collective-permute-start(bf16[64,1024]{1,0:T(8,128)(2,1)} %fusion.49), channel_id=1, source_target_pairs={{96,32},{97,33},{98,34},{99,35},{100,36},{101,37},{102,38},{103,39... | collective-permute-start | bytes 393224 | tf_op jit(solution)/shard_map/ppermute | solution.py:26
  69.1 35.1 %collective-permute-start.21 = (bf16[4,128,1024]{2,1,0:T(8,128)(2,1)}, bf16[4,128,1024]{2,1,0:T(8,128)(2,1)S(1)}, u32[]{:S(2)}, u32[]{:S(2)}) collective-permute-start(bf16[4,128,1024]{2,1,0:T(8,128)(2,1)} %get-tuple-element.33), channel_id=1, source_target_pairs={{0,1},{1,0},{2,3},{3,2},{4,5},{5,4},{6,7},{7,6},{8,9},{9,8},{10,11... | collective-permute-start | bytes 3145736 | tf_op jit(solution)/shard_map/ppermute | solution.py:22
  86.8 16.2 %collective-permute-start.16 = (bf16[128,1024]{1,0:T(8,128)(2,1)}, bf16[128,1024]{1,0:T(8,128)(2,1)}, u32[]{:S(2)}, u32[]{:S(2)}) collective-permute-start(bf16[128,1024]{1,0:T(8,128)(2,1)} %fusion.18), channel_id=1, source_target_pairs={{0,16},{8,24},{16,0},{24,8},{1,17},{9,25},{17,1},{25,9},{2,18},{10... | collective-permute-start | bytes 786440 | tf_op jit(solution)/shard_map/ppermute | solution.py:22
  124.9 21.4 %collective-permute-start.32 = (f32[4,128,1024]{2,1,0:T(8,128)S(1)}, f32[4,128,1024]{2,1,0:T(8,128)S(1)}, u32[]{:S(2)}, u32[]{:S(2)}) collective-permute-start(f32[4,128,1024]{2,1,0:T(8,128)S(1)} %bitcast.133), channel_id=1, source_target_pairs={{0,1},{1,0},{2,3},{3,2},{4,5},{5,4},{6,7},{7,6},{8,9},{9,8},{10,11... | collective-permute-start | bytes 6291464 | tf_op jit(solution)/shard_map/ppermute | solution.py:22
  125.1 15.6 %collective-permute-start.26 = (f16[128,1024]{1,0:T(8,128)(2,1)S(1)}, f16[128,1024]{1,0:T(8,128)(2,1)S(1)}, u32[]{:S(2)}, u32[]{:S(2)}) collective-permute-start(f16[128,1024]{1,0:T(8,128)(2,1)S(1)} %get-tuple-element.24), channel_id=1, source_target_pairs={{0,8},{8,16},{16,24},{24,0},{1,9},{9,17},{17,25},{25,1},{2,10},{10... | collective-permute-start | bytes 786440 | tf_op jit(solution)/shard_map/ppermute | solution.py:22
  125.7 15.0 %collective-permute-start.28 = (f16[128,1024]{1,0:T(8,128)(2,1)S(1)}, f16[128,1024]{1,0:T(8,128)(2,1)S(1)}, u32[]{:S(2)}, u32[]{:S(2)}) collective-permute-start(f16[128,1024]{1,0:T(8,128)(2,1)S(1)} %get-tuple-element.25), channel_id=1, source_target_pairs={{0,24},{8,0},{16,8},{24,16},{1,25},{9,1},{17,9},{25,17},{2,26},{10... | collective-permute-start | bytes 786440 | tf_op jit(solution)/shard_map/ppermute | solution.py:22
  142.3 13.5 %collective-permute-start.29 = (f16[128,1024]{1,0:T(8,128)(2,1)S(1)}, f16[128,1024]{1,0:T(8,128)(2,1)S(1)}, u32[]{:S(2)}, u32[]{:S(2)}) collective-permute-start(f16[128,1024]{1,0:T(8,128)(2,1)S(1)} %add_convert_fusion), channel_id=1, source_target_pairs={{0,96},{1,97},{2,98},{3,99},{4,100},{5,101},{6,102},{7,103},{8,104... | collective-permute-start | bytes 786440 | tf_op jit(solution)/shard_map/ppermute | solution.py:26
  172.3 17.7 %collective-permute-start.47 = (bf16[4,128,512]{2,1,0:T(8,128)(2,1)S(1)}, bf16[4,128,512]{2,1,0:T(8,128)(2,1)S(1)}, u32[]{:S(2)}, u32[]{:S(2)}) collective-permute-start(bf16[4,128,512]{2,1,0:T(8,128)(2,1)S(1)} %pad_maximum_fusion.3.refs_8_), channel_id=1, source_target_pairs={{0,8},{8,0},{1,9},{9,1},{2,10},{10,2},{3,11},{11,3},{4,12},{12,4},... | collective-permute-start | bytes 1572872 | tf_op jit(solution)/shard_map/ppermute | solution.py:22
  186.6 15.5 %collective-permute-start.39 = (bf16[2,128,512]{2,1,0:T(8,128)(2,1)S(1)}, bf16[2,128,512]{2,1,0:T(8,128)(2,1)S(1)}, u32[]{:S(2)}, u32[]{:S(2)}) collective-permute-start(bf16[2,128,512]{2,1,0:T(8,128)(2,1)S(1)} %pad_maximum_fusion.5.refs_0_), channel_id=1, source_target_pairs={{0,2},{2,4},{4,6},{6,0},{1,3},{3,5},{5,7},{7,1},{8,10},{10,12},{12... | collective-permute-start | bytes 786440 | tf_op jit(solution)/shard_map/ppermute | solution.py:22
  186.6 15.5 %collective-permute-start.38 = (bf16[2,128,512]{2,1,0:T(8,128)(2,1)S(1)}, bf16[2,128,512]{2,1,0:T(8,128)(2,1)S(1)}, u32[]{:S(2)}, u32[]{:S(2)}) collective-permute-start(bf16[2,128,512]{2,1,0:T(8,128)(2,1)S(1)} %pad_maximum_fusion.5.refs_0_), channel_id=1, source_target_pairs={{0,4},{2,6},{4,0},{6,2},{1,5},{3,7},{5,1},{7,3},{8,12},{10,14},{12... | collective-permute-start | bytes 786440 | tf_op jit(solution)/shard_map/ppermute | solution.py:22
  187.9 15.1 %collective-permute-start.48 = (bf16[4,128,512]{2,1,0:T(8,128)(2,1)S(1)}, bf16[4,128,512]{2,1,0:T(8,128)(2,1)S(1)}, u32[]{:S(2)}, u32[]{:S(2)}) collective-permute-start(bf16[4,128,512]{2,1,0:T(8,128)(2,1)S(1)} %pad_maximum_fusion.3.refs_8_), channel_id=1, source_target_pairs={{0,1},{1,0},{2,3},{3,2},{4,5},{5,4},{6,7},{7,6},{8,9},{9,8},{10,11... | collective-permute-start | bytes 1572872 | tf_op jit(solution)/shard_map/ppermute | solution.py:22
  188.1 14.6 %collective-permute-start.37 = (bf16[2,128,512]{2,1,0:T(8,128)(2,1)S(1)}, bf16[2,128,512]{2,1,0:T(8,128)(2,1)S(1)}, u32[]{:S(2)}, u32[]{:S(2)}) collective-permute-start(bf16[2,128,512]{2,1,0:T(8,128)(2,1)S(1)} %pad_maximum_fusion.5.refs_0_), channel_id=1, source_target_pairs={{0,6},{2,0},{4,2},{6,4},{1,7},{3,1},{5,3},{7,5},{8,14},{10,8},{12,... | collective-permute-start | bytes 786440 | tf_op jit(solution)/shard_map/ppermute | solution.py:22
  190.0 14.4 %collective-permute-start.49 = (bf16[4,128,512]{2,1,0:T(8,128)(2,1)S(1)}, bf16[4,128,512]{2,1,0:T(8,128)(2,1)S(1)}, u32[]{:S(2)}, u32[]{:S(2)}) collective-permute-start(bf16[4,128,512]{2,1,0:T(8,128)(2,1)S(1)} %collective-permute-done.47.refs_9_), channel_id=1, source_target_pairs={{0,1},{1,0},{2,3},{3,2},{4,5},{5,4},{6,7},{7,6},{8,9},{9,8},{10,11... | collective-permute-start | bytes 1572872 | tf_op jit(solution)/shard_map/ppermute | solution.py:22
  230.0 20.1 %all-to-all-start.3 = ((bf16[8,2,32,1024]{3,2,1,0:T(8,128)(2,1)}), bf16[8,2,32,1024]{3,2,1,0:T(8,128)(2,1)S(1)}, u32[]{:S(2)}, u32[]{:S(2)}) async-start(bf16[8,2,32,1024]{3,2,1,0:T(8,128)(2,1)} %shard_map.76), calls=%async_computation.3 | async-start | bytes 2097152 | tf_op jit(solution)/shard_map/all_to_all | solution.py:245
  (45 other events, 389.7 us)

commit v3 on v2

--- a/solution.py
+++ b/solution.py
@@ -29,6 +29,11 @@
 def turned(array, shift):
     n = array.shape[0]
     return lax.dynamic_slice_in_dim(jnp.concatenate([array, array]), shift, n, 0)
+
+
+def part(array, index, count):
+    size = array.shape[0] // count
+    return lax.dynamic_slice_in_dim(array, index * size, size, 0)
 
 
 def row_order_kernel(at, *refs):
@@ -124,17 +129,15 @@
     outer = lax.ppermute(weight, Y, [(k, 3 - k) for k in range(4)])
     other = fetch(weight, "c", 1)
     outer_other = fetch(outer, "c", 1)
-    mine = features.reshape(4, rows // 4, feats)
-    mine = lax.all_to_all(mine, ("yl", "c"), 0, 0, tiled=True)
-    sources = ((2 * yl + c, weight), (2 * yl + 1 - c, other))
-    sources += ((2 - 2 * yl + c, outer), (3 - 2 * yl - c, outer_other))
+    mine = [part(features, 2 * yl + c, 4)]
+    mine.append(fetch(part(features, 2 * yl + 1 - c, 4), "c", 1))
+    mine.append(fetch(part(features, 2 - 2 * yl + c, 4), "yl", 1))
+    mine.append(
+        lax.ppermute(part(features, 3 - 2 * yl - c, 4), ("yl", "c"), [(k, 3 - k) for k in range(4)])
+    )
     partial = sum(
-        jnp.dot(
-            lax.dynamic_index_in_dim(mine, k, 0, keepdims=False),
-            w,
-            preferred_element_type=jnp.float32,
-        )
-        for k, w in sources
+        jnp.dot(f, w, preferred_element_type=jnp.float32)
+        for f, w in zip(mine, (weight, other, outer, outer_other))
     )
     halves = partial.reshape(4, 2, per // 2, emb)
 
@@ -196,6 +199,7 @@
 
     probs = jnp.where(live, jnp.exp(logits - lse_rows[:, None]), 0.0)
     dlogit = ((probs - hit.astype(jnp.float32)) / total_q).astype(jnp.bfloat16)
+    dlogit = lax.optimization_barrier(dlogit)
     dquery = jnp.dot(dlogit, passages, preferred_element_type=jnp.float32)
     dpassage = lax.dot_general(
         dlogit, queries, (((0,), (0,)), ((), ())), preferred_element_type=jnp.float32

time: 254 us -> 257 us (1.012)
  blocking collectives: 32.9 us -> 42.5 us
  starting transfers between devices: 63.7 us -> 57.5 us
    all_to_all x1, blocking collectives: 21.7 us -> 26.9 us  [local(): lax.all_to_all(weight_part.reshape(8, feats // 8, emb), ('grp', 'dp'), 0,...]
    all_to_all x1, blocking collectives: 11.2 us -> 15.6 us  [local(): lax.all_to_all(jnp.broadcast_to(stats.reshape(1, 12, per), (16, 12, per))...]
    ppermute x40 -> x42, waiting for transfers between devices: 91.4 us -> 95.1 us  [fetch(): lax.ppermute(array, axis, [(k, (k - step) % size) for k in range(size)])]
    all_to_all x1 -> x0, starting transfers between devices: 3.66 us -> none  [local(): mine = lax.all_to_all(mine, ('yl', 'c'), 0, 0, tiled=True)]
    ppermute x1, waiting for transfers between devices: 12.2 us -> 8.58 us  [local(): outer = lax.ppermute(weight, Y, [(k, 3 - k) for k in range(4)])]
    ppermute x40 -> x42, starting transfers between devices: 40.7 us -> 39.8 us  [fetch(): lax.ppermute(array, axis, [(k, (k - step) % size) for k in range(size)])]
  transfers between devices with their start and end apart: 52 -> 54, of which waited for: 31 -> 28; matrix products, arithmetic and copies ran while one was open for 7% -> 6% of each run, Pallas kernels for 0% -> 0%
where the time goes in v3:
time: 257 us; the launch traced here: 256 us
  waiting for transfers between devices  119 us (46%)
  starting transfers between devices  57.5 us (22%)
  blocking collectives  42.5 us (17%)
  matrix products  13.4 us (5%)
  other arithmetic  12.6 us (5%)
  local copies, waits for them, and re-layouts  4.35 us (2%)
  Pallas kernels  3.33 us (1%)
  between operations  3.09 us (1%)
    ppermute x42, waiting for transfers between devices, fetch(): lax.ppermute(array, axis, [(k, (k - step) % size) for k in range(size)])  95.1 us
    ppermute x42, starting transfers between devices, fetch(): lax.ppermute(array, axis, [(k, (k - step) % size) for k in range(size)])  39.8 us
    all_to_all x1, blocking collectives, local(): lax.all_to_all(weight_part.reshape(8, feats // 8, emb), ('grp', 'dp'), 0,...  26.9 us
    all_to_all x1, blocking collectives, local(): lax.all_to_all(jnp.broadcast_to(stats.reshape(1, 12, per), (16, 12, per))...  15.6 us
    ppermute x9, waiting for transfers between devices, one_way(): return lax.ppermute(array, axis, [(source, target)])  14.4 us
    ppermute x9, starting transfers between devices, one_way(): return lax.ppermute(array, axis, [(source, target)])  9.39 us
    ppermute x1, waiting for transfers between devices, local(): outer = lax.ppermute(weight, Y, [(k, 3 - k) for k in range(4)])  8.58 us
  transfers between devices with their start and end apart: 54, of which 28 were waited for; matrix products, arithmetic and copies ran while one was open for 6% of the time, Pallas kernels for 0%

profile of v3, /device:TPU:0, one launch (start us, length us, event | category | flops | bytes accessed | tf_op | source)
XLA Modules:
  0.0 256.0 jit_solution(7877680794314399819)
XLA Ops:
  1.9 3.2 %collective-permute-start.3 = (bf16[256,1024]{1,0:T(8,128)(2,1)S(1)}, bf16[256,1024]{1,0:T(8,128)(2,1)S(1)}, u32[]{:S(2)}, u32[]{:S(2)}) collective-permute-start(bf16[256,1024]{1,0:T(8,128)(2,1)S(1)} %broadcast_select_fusion), channel_id=1, source_target_pairs={{0,24},{8,16},{16,8},{24,0},{1,25},{9,17},{17,9},{25,1},{2,26},{10... | collective-permute-start | bytes 1572872 | tf_op jit(solution)/shard_map/ppermute | solution.py:129
  8.4 8.6 %collective-permute-done.3 = bf16[256,1024]{1,0:T(8,128)(2,1)S(1)} collective-permute-done((bf16[256,1024]{1,0:T(8,128)(2,1)S(1)}, bf16[256,1024]{1,0:T(8,128)(2,1)S(1)}, u32[]{:S(2)}, u32[]{:S(2)}) %collective-permute-start.3) | collective-permute-done | bytes 524320 | tf_op jit(solution)/shard_map/ppermute | solution.py:129
  20.7 2.8 %collective-permute-start.6 = (f32[64,1024]{1,0:T(8,128)S(1)}, f32[64,1024]{1,0:T(8,128)}, u32[]{:S(2)}, u32[]{:S(2)}) collective-permute-start(f32[64,1024]{1,0:T(8,128)S(1)} %get-tuple-element.36), channel_id=1, source_target_pairs={{0,6},{2,0},{4,2},{6,4},{1,7},{3,1},{5,3},{7,5},{8,14},{10,8},{12,... | collective-permute-start | bytes 786440 | tf_op jit(solution)/shard_map/ppermute | solution.py:22
  28.6 12.4 %collective-permute-done.6 = f32[64,1024]{1,0:T(8,128)} collective-permute-done((f32[64,1024]{1,0:T(8,128)S(1)}, f32[64,1024]{1,0:T(8,128)}, u32[]{:S(2)}, u32[]{:S(2)}) %collective-permute-start.6) | collective-permute-done | bytes 262176 | tf_op jit(solution)/shard_map/ppermute | solution.py:22
  41.0 3.8 %collective-permute-start.9 = (f32[64,1024]{1,0:T(8,128)S(1)}, f32[64,1024]{1,0:T(8,128)S(1)}, u32[]{:S(2)}, u32[]{:S(2)}) collective-permute-start(f32[64,1024]{1,0:T(8,128)S(1)} %get-tuple-element.39), channel_id=1, source_target_pairs={{0,6},{2,0},{4,2},{6,4},{1,7},{3,1},{5,3},{7,5},{8,14},{10,8},{12,... | collective-permute-start | bytes 786440 | tf_op jit(solution)/shard_map/ppermute | solution.py:22
  46.1 4.2 %collective-permute-done.11 = f32[64,1024]{1,0:T(8,128)S(1)} collective-permute-done((f32[64,1024]{1,0:T(8,128)S(1)}, f32[64,1024]{1,0:T(8,128)S(1)}, u32[]{:S(2)}, u32[]{:S(2)}) %collective-permute-start.11) | collective-permute-done | bytes 262176 | tf_op jit(solution)/shard_map/ppermute | solution.py:22
  51.1 3.5 %collective-permute-start.21 = (bf16[128,1024]{1,0:T(8,128)(2,1)S(1)}, bf16[128,1024]{1,0:T(8,128)(2,1)S(1)}, u32[]{:S(2)}, u32[]{:S(2)}) collective-permute-start(bf16[128,1024]{1,0:T(8,128)(2,1)S(1)} %pad_maximum_fusion.4), channel_id=1, source_target_pairs={{0,6},{2,0},{4,2},{6,4},{1,7},{3,1},{5,3},{7,5},{8,14},{10,8},{12,... | collective-permute-start | bytes 786440 | tf_op jit(solution)/shard_map/ppermute | solution.py:22
  57.5 7.1 %collective-permute-done.21 = bf16[128,1024]{1,0:T(8,128)(2,1)S(1)} collective-permute-done((bf16[128,1024]{1,0:T(8,128)(2,1)S(1)}, bf16[128,1024]{1,0:T(8,128)(2,1)S(1)}, u32[]{:S(2)}, u32[]{:S(2)}) %collective-permute-start.21) | collective-permute-done | bytes 262176 | tf_op jit(solution)/shard_map/ppermute | solution.py:22
  72.7 8.1 %collective-permute-done.13 = bf16[64,1024]{1,0:T(8,128)(2,1)S(1)} collective-permute-done((bf16[64,1024]{1,0:T(8,128)(2,1)S(1)}, bf16[64,1024]{1,0:T(8,128)(2,1)S(1)}, u32[]{:S(2)}, u32[]{:S(2)}) %collective-permute-start.13) | collective-permute-done | bytes 131104 | tf_op jit(solution)/shard_map/ppermute | solution.py:26
  81.8 3.2 %collective-permute-start.18 = (bf16[128,1024]{1,0:T(8,128)(2,1)S(1)}, bf16[128,1024]{1,0:T(8,128)(2,1)S(1)}, u32[]{:S(2)}, u32[]{:S(2)}) collective-permute-start(bf16[128,1024]{1,0:T(8,128)(2,1)S(1)} %fusion.18), channel_id=1, source_target_pairs={{0,24},{8,0},{16,8},{24,16},{1,25},{9,1},{17,9},{25,17},{2,26},{10... | collective-permute-start | bytes 786440 | tf_op jit(solution)/shard_map/ppermute | solution.py:22
  86.0 9.9 %collective-permute-done.18 = bf16[128,1024]{1,0:T(8,128)(2,1)S(1)} collective-permute-done((bf16[128,1024]{1,0:T(8,128)(2,1)S(1)}, bf16[128,1024]{1,0:T(8,128)(2,1)S(1)}, u32[]{:S(2)}, u32[]{:S(2)}) %collective-permute-start.18) | collective-permute-done | bytes 262176 | tf_op jit(solution)/shard_map/ppermute | solution.py:22
  96.0 3.4 %collective-permute-done.20 = bf16[128,1024]{1,0:T(8,128)(2,1)S(1)} collective-permute-done((bf16[128,1024]{1,0:T(8,128)(2,1)S(1)}, bf16[128,1024]{1,0:T(8,128)(2,1)S(1)}, u32[]{:S(2)}, u32[]{:S(2)}) %collective-permute-start.20) | collective-permute-done | bytes 262176 | tf_op jit(solution)/shard_map/ppermute | solution.py:22
  103.8 15.6 %all_to_all.15 = f32[16,12,128]{2,1,0:T(8,128)S(1)} all-to-all(f32[16,12,128]{2,1,0:T(8,128)S(1)} %broadcast_in_dim.36), channel_id=1, replica_groups=mesh['grp'=4,'dp'=2,'yl'=2,'x'=4,'c'=2] {'grp','dp','yl'}, dimensions={0} | all-to-all | bytes 196608 | tf_op jit(solution)/shard_map/all_to_all | solution.py:186
  128.4 11.7 %collective-permute-done.29 = f16[128,1024]{1,0:T(8,128)(2,1)S(1)} collective-permute-done((f16[128,1024]{1,0:T(8,128)(2,1)S(1)}, f16[128,1024]{1,0:T(8,128)(2,1)S(1)}, u32[]{:S(2)}, u32[]{:S(2)}) %collective-permute-start.29) | collective-permute-done | bytes 262176 | tf_op jit(solution)/shard_map/ppermute | solution.py:22
  148.1 6.3 %collective-permute-done.32 = f16[128,1024]{1,0:T(8,128)(2,1)S(1)} collective-permute-done((f16[128,1024]{1,0:T(8,128)(2,1)S(1)}, f16[128,1024]{1,0:T(8,128)(2,1)S(1)}, u32[]{:S(2)}, u32[]{:S(2)}) %collective-permute-start.32) | collective-permute-done | bytes 262176 | tf_op jit(solution)/shard_map/ppermute | solution.py:26
  155.3 4.6 %collective-permute-done.36 = f16[128,1024]{1,0:T(8,128)(2,1)S(1)} collective-permute-done((f16[128,1024]{1,0:T(8,128)(2,1)S(1)}, f16[128,1024]{1,0:T(8,128)(2,1)S(1)}, u32[]{:S(2)}, u32[]{:S(2)}) %collective-permute-start.36) | collective-permute-done | bytes 262176 | tf_op jit(solution)/shard_map/ppermute | solution.py:22
  165.1 3.0 %collective-permute-done.47 = bf16[128,512]{1,0:T(8,128)(2,1)S(1)} collective-permute-done((bf16[128,512]{1,0:T(8,128)(2,1)S(1)}, bf16[128,512]{1,0:T(8,128)(2,1)S(1)}, u32[]{:S(2)}, u32[]{:S(2)}) %collective-permute-start.47) | collective-permute-done | bytes 131104 | tf_op jit(solution)/shard_map/ppermute | solution.py:22
  174.2 11.7 %collective-permute-done.39 = bf16[128,512]{1,0:T(8,128)(2,1)S(1)} collective-permute-done((bf16[128,512]{1,0:T(8,128)(2,1)S(1)}, bf16[128,512]{1,0:T(8,128)(2,1)S(1)}, u32[]{:S(2)}, u32[]{:S(2)}) %collective-permute-start.39) | collective-permute-done | bytes 131104 | tf_op jit(solution)/shard_map/ppermute | solution.py:22
  188.7 4.8 %collective-permute-done.40.refs_1_ = bf16[2,128,512]{2,1,0:T(8,128)(2,1)S(1)} collective-permute-done((bf16[2,128,512]{2,1,0:T(8,128)(2,1)S(1)}, bf16[2,128,512]{2,1,0:T(8,128)(2,1)S(1)}, u32[]{:S(2)}, u32[]{:S(2)}) %collective-permute-start.40) | collective-permute-done | bytes 262176 | tf_op jit(solution)/shard_map/ppermute | solution.py:22
  194.0 3.1 %collective-permute-done.41.refs_2_ = bf16[2,128,512]{2,1,0:T(8,128)(2,1)S(1)} collective-permute-done((bf16[2,128,512]{2,1,0:T(8,128)(2,1)S(1)}, bf16[2,128,512]{2,1,0:T(8,128)(2,1)S(1)}, u32[]{:S(2)}, u32[]{:S(2)}) %collective-permute-start.41) | collective-permute-done | bytes 262176 | tf_op jit(solution)/shard_map/ppermute | solution.py:22
  197.1 3.7 %collective-permute-done.42.refs_3_ = bf16[2,128,512]{2,1,0:T(8,128)(2,1)S(1)} collective-permute-done((bf16[2,128,512]{2,1,0:T(8,128)(2,1)S(1)}, bf16[2,128,512]{2,1,0:T(8,128)(2,1)S(1)}, u32[]{:S(2)}, u32[]{:S(2)}) %collective-permute-start.42) | collective-permute-done | bytes 262176 | tf_op jit(solution)/shard_map/ppermute | solution.py:22
  205.6 26.9 %all_to_all.16.share = f32[8,32,1024]{2,1,0:T(8,128)S(1)} all-to-all(f32[8,32,1024]{2,1,0:T(8,128)S(1)} %bitcast.137), channel_id=1, replica_groups=mesh['grp'=4,'dp'=2,'yl'=2,'x'=4,'c'=2] {'grp','dp'}, dimensions={0} | all-to-all | bytes 2097152 | tf_op jit(solution)/shard_map/all_to_all | solution.py:246
  233.6 3.6 %all-to-all-start.2 = ((bf16[8,2,32,1024]{3,2,1,0:T(8,128)(2,1)}), bf16[8,2,32,1024]{3,2,1,0:T(8,128)(2,1)S(1)}, u32[]{:S(2)}, u32[]{:S(2)}) async-start(bf16[8,2,32,1024]{3,2,1,0:T(8,128)(2,1)} %shard_map.76), calls=%async_computation.2 | async-start | bytes 2097152 | tf_op jit(solution)/shard_map/all_to_all | solution.py:249
  247.9 4.5 %fusion = bf16[1,2048,256]{2,1,0:T(8,128)(2,1)} fusion(bf16[2048,1024]{1,0:T(8,128)(2,1)} %copy-done.2, bf16[256,1024]{1,0:T(8,128)(2,1)S(1)} %broadcast_select_fusion), kind=kOutput, calls=%fused_computation.3 | convolution fusion | flops 1074266112 | bytes 5767168 | tf_op jit(solution)/shard_map/dot_general | solution.py:242
  (180 shorter events, 83.2 us)
Async XLA Ops:
  1.9 15.1 %collective-permute-start.3 = (bf16[256,1024]{1,0:T(8,128)(2,1)S(1)}, bf16[256,1024]{1,0:T(8,128)(2,1)S(1)}, u32[]{:S(2)}, u32[]{:S(2)}) collective-permute-start(bf16[256,1024]{1,0:T(8,128)(2,1)S(1)} %broadcast_select_fusion), channel_id=1, source_target_pairs={{0,24},{8,16},{16,8},{24,0},{1,25},{9,17},{17,9},{25,1},{2,26},{10... | collective-permute-start | bytes 1572872 | tf_op jit(solution)/shard_map/ppermute | solution.py:129
  6.3 13.6 %collective-permute-start.4 = (bf16[512,256]{1,0:T(8,128)(2,1)S(1)}, bf16[512,256]{1,0:T(8,128)(2,1)S(1)}, u32[]{:S(2)}, u32[]{:S(2)}) collective-permute-start(bf16[512,256]{1,0:T(8,128)(2,1)S(1)} %get-tuple-element.40), channel_id=1, source_target_pairs={{0,9},{1,8},{8,1},{9,0},{2,11},{3,10},{10,3},{11,2},{4,13},{5,12},... | collective-permute-start | bytes 786440 | tf_op jit(solution)/shard_map/ppermute | solution.py:136
  20.7 20.2 %collective-permute-start.6 = (f32[64,1024]{1,0:T(8,128)S(1)}, f32[64,1024]{1,0:T(8,128)}, u32[]{:S(2)}, u32[]{:S(2)}) collective-permute-start(f32[64,1024]{1,0:T(8,128)S(1)} %get-tuple-element.36), channel_id=1, source_target_pairs={{0,6},{2,0},{4,2},{6,4},{1,7},{3,1},{5,3},{7,5},{8,14},{10,8},{12,... | collective-permute-start | bytes 786440 | tf_op jit(solution)/shard_map/ppermute | solution.py:22
  23.6 21.2 %collective-permute-start.7 = (f32[64,1024]{1,0:T(8,128)S(1)}, f32[64,1024]{1,0:T(8,128)}, u32[]{:S(2)}, u32[]{:S(2)}) collective-permute-start(f32[64,1024]{1,0:T(8,128)S(1)} %get-tuple-element.34), channel_id=1, source_target_pairs={{0,4},{2,6},{4,0},{6,2},{1,5},{3,7},{5,1},{7,3},{8,12},{10,14},{12... | collective-permute-start | bytes 786440 | tf_op jit(solution)/shard_map/ppermute | solution.py:22
  24.4 20.4 %collective-permute-start.8 = (f32[64,1024]{1,0:T(8,128)S(1)}, f32[64,1024]{1,0:T(8,128)}, u32[]{:S(2)}, u32[]{:S(2)}) collective-permute-start(f32[64,1024]{1,0:T(8,128)S(1)} %get-tuple-element.35), channel_id=1, source_target_pairs={{0,2},{2,4},{4,6},{6,0},{1,3},{3,5},{5,7},{7,1},{8,10},{10,12},{12... | collective-permute-start | bytes 786440 | tf_op jit(solution)/shard_map/ppermute | solution.py:22
  25.3 20.7 %collective-permute-start.10 = (f32[64,1024]{1,0:T(8,128)S(1)}, f32[64,1024]{1,0:T(8,128)S(1)}, u32[]{:S(2)}, u32[]{:S(2)}) collective-permute-start(f32[64,1024]{1,0:T(8,128)S(1)} %get-tuple-element.37), channel_id=1, source_target_pairs={{0,4},{2,6},{4,0},{6,2},{1,5},{3,7},{5,1},{7,3},{8,12},{10,14},{12... | collective-permute-start | bytes 786440 | tf_op jit(solution)/shard_map/ppermute | solution.py:22
  27.2 23.0 %collective-permute-start.11 = (f32[64,1024]{1,0:T(8,128)S(1)}, f32[64,1024]{1,0:T(8,128)S(1)}, u32[]{:S(2)}, u32[]{:S(2)}) collective-permute-start(f32[64,1024]{1,0:T(8,128)S(1)} %get-tuple-element.38), channel_id=1, source_target_pairs={{0,2},{2,4},{4,6},{6,0},{1,3},{3,5},{5,7},{7,1},{8,10},{10,12},{12... | collective-permute-start | bytes 786440 | tf_op jit(solution)/shard_map/ppermute | solution.py:22
  51.1 13.6 %collective-permute-start.21 = (bf16[128,1024]{1,0:T(8,128)(2,1)S(1)}, bf16[128,1024]{1,0:T(8,128)(2,1)S(1)}, u32[]{:S(2)}, u32[]{:S(2)}) collective-permute-start(bf16[128,1024]{1,0:T(8,128)(2,1)S(1)} %pad_maximum_fusion.4), channel_id=1, source_target_pairs={{0,6},{2,0},{4,2},{6,4},{1,7},{3,1},{5,3},{7,5},{8,14},{10,8},{12,... | collective-permute-start | bytes 786440 | tf_op jit(solution)/shard_map/ppermute | solution.py:22
  54.6 13.5 %collective-permute-start.23 = (bf16[128,1024]{1,0:T(8,128)(2,1)S(1)}, bf16[128,1024]{1,0:T(8,128)(2,1)S(1)}, u32[]{:S(2)}, u32[]{:S(2)}) collective-permute-start(bf16[128,1024]{1,0:T(8,128)(2,1)S(1)} %pad_maximum_fusion.4), channel_id=1, source_target_pairs={{0,2},{2,4},{4,6},{6,0},{1,3},{3,5},{5,7},{7,1},{8,10},{10,12},{12... | collective-permute-start | bytes 786440 | tf_op jit(solution)/shard_map/ppermute | solution.py:22
  55.6 15.6 %collective-permute-start.12 = (bf16[64,1024]{1,0:T(8,128)(2,1)S(1)}, bf16[64,1024]{1,0:T(8,128)(2,1)S(1)}, u32[]{:S(2)}, u32[]{:S(2)}) collective-permute-start(bf16[64,1024]{1,0:T(8,128)(2,1)S(1)} %fusion.38), channel_id=1, source_target_pairs={{96,0},{97,1},{98,2},{99,3},{100,4},{101,5},{102,6},{103,7},{104,8... | collective-permute-start | bytes 393224 | tf_op jit(solution)/shard_map/ppermute | solution.py:26
  56.9 15.0 %collective-permute-start.14 = (bf16[64,1024]{1,0:T(8,128)(2,1)S(1)}, bf16[64,1024]{1,0:T(8,128)(2,1)S(1)}, u32[]{:S(2)}, u32[]{:S(2)}) collective-permute-start(bf16[64,1024]{1,0:T(8,128)(2,1)S(1)} %fusion.38), channel_id=1, source_target_pairs={{96,32},{97,33},{98,34},{99,35},{100,36},{101,37},{102,38},{103,39... | collective-permute-start | bytes 393224 | tf_op jit(solution)/shard_map/ppermute | solution.py:26
  69.2 30.3 %collective-permute-start.24 = (bf16[4,128,1024]{2,1,0:T(8,128)(2,1)}, bf16[4,128,1024]{2,1,0:T(8,128)(2,1)}, u32[]{:S(2)}, u32[]{:S(2)}) collective-permute-start(bf16[4,128,1024]{2,1,0:T(8,128)(2,1)} %get-tuple-element.33), channel_id=1, source_target_pairs={{0,1},{1,0},{2,3},{3,2},{4,5},{5,4},{6,7},{7,6},{8,9},{9,8},{10,11... | collective-permute-start | bytes 3145736 | tf_op jit(solution)/shard_map/ppermute | solution.py:22
  81.8 14.2 %collective-permute-start.18 = (bf16[128,1024]{1,0:T(8,128)(2,1)S(1)}, bf16[128,1024]{1,0:T(8,128)(2,1)S(1)}, u32[]{:S(2)}, u32[]{:S(2)}) collective-permute-start(bf16[128,1024]{1,0:T(8,128)(2,1)S(1)} %fusion.18), channel_id=1, source_target_pairs={{0,24},{8,0},{16,8},{24,16},{1,25},{9,1},{17,9},{25,17},{2,26},{10... | collective-permute-start | bytes 786440 | tf_op jit(solution)/shard_map/ppermute | solution.py:22
  85.0 14.4 %collective-permute-start.20 = (bf16[128,1024]{1,0:T(8,128)(2,1)S(1)}, bf16[128,1024]{1,0:T(8,128)(2,1)S(1)}, u32[]{:S(2)}, u32[]{:S(2)}) collective-permute-start(bf16[128,1024]{1,0:T(8,128)(2,1)S(1)} %fusion.18), channel_id=1, source_target_pairs={{0,8},{8,16},{16,24},{24,0},{1,9},{9,17},{17,25},{25,1},{2,10},{10... | collective-permute-start | bytes 786440 | tf_op jit(solution)/shard_map/ppermute | solution.py:22
  124.3 20.8 %collective-permute-start.35 = (f32[4,128,1024]{2,1,0:T(8,128)S(1)}, f32[4,128,1024]{2,1,0:T(8,128)S(1)}, u32[]{:S(2)}, u32[]{:S(2)}) collective-permute-start(f32[4,128,1024]{2,1,0:T(8,128)S(1)} %bitcast.136), channel_id=1, source_target_pairs={{0,1},{1,0},{2,3},{3,2},{4,5},{5,4},{6,7},{7,6},{8,9},{9,8},{10,11... | collective-permute-start | bytes 6291464 | tf_op jit(solution)/shard_map/ppermute | solution.py:22
  124.5 15.6 %collective-permute-start.29 = (f16[128,1024]{1,0:T(8,128)(2,1)S(1)}, f16[128,1024]{1,0:T(8,128)(2,1)S(1)}, u32[]{:S(2)}, u32[]{:S(2)}) collective-permute-start(f16[128,1024]{1,0:T(8,128)(2,1)S(1)} %get-tuple-element.24), channel_id=1, source_target_pairs={{0,8},{8,16},{16,24},{24,0},{1,9},{9,17},{17,25},{25,1},{2,10},{10... | collective-permute-start | bytes 786440 | tf_op jit(solution)/shard_map/ppermute | solution.py:22
  125.2 15.0 %collective-permute-start.30 = (f16[128,1024]{1,0:T(8,128)(2,1)S(1)}, f16[128,1024]{1,0:T(8,128)(2,1)S(1)}, u32[]{:S(2)}, u32[]{:S(2)}) collective-permute-start(f16[128,1024]{1,0:T(8,128)(2,1)S(1)} %get-tuple-element.26), channel_id=1, source_target_pairs={{0,16},{8,24},{16,0},{24,8},{1,17},{9,25},{17,1},{25,9},{2,18},{10... | collective-permute-start | bytes 786440 | tf_op jit(solution)/shard_map/ppermute | solution.py:22
  127.0 13.8 %collective-permute-start.31 = (f16[128,1024]{1,0:T(8,128)(2,1)S(1)}, f16[128,1024]{1,0:T(8,128)(2,1)S(1)}, u32[]{:S(2)}, u32[]{:S(2)}) collective-permute-start(f16[128,1024]{1,0:T(8,128)(2,1)S(1)} %get-tuple-element.25), channel_id=1, source_target_pairs={{0,24},{8,0},{16,8},{24,16},{1,25},{9,1},{17,9},{25,17},{2,26},{10... | collective-permute-start | bytes 786440 | tf_op jit(solution)/shard_map/ppermute | solution.py:22
  141.0 13.5 %collective-permute-start.32 = (f16[128,1024]{1,0:T(8,128)(2,1)S(1)}, f16[128,1024]{1,0:T(8,128)(2,1)S(1)}, u32[]{:S(2)}, u32[]{:S(2)}) collective-permute-start(f16[128,1024]{1,0:T(8,128)(2,1)S(1)} %add_convert_fusion), channel_id=1, source_target_pairs={{0,96},{1,97},{2,98},{3,99},{4,100},{5,101},{6,102},{7,103},{8,104... | collective-permute-start | bytes 786440 | tf_op jit(solution)/shard_map/ppermute | solution.py:26
  145.7 14.2 %collective-permute-start.36 = (f16[128,1024]{1,0:T(8,128)(2,1)S(1)}, f16[128,1024]{1,0:T(8,128)(2,1)S(1)}, u32[]{:S(2)}, u32[]{:S(2)}) collective-permute-start(f16[128,1024]{1,0:T(8,128)(2,1)S(1)} %get-tuple-element.27), channel_id=1, source_target_pairs={{0,2},{2,4},{4,6},{6,0},{1,3},{3,5},{5,7},{7,1},{8,10},{10,12},{12... | collective-permute-start | bytes 786440 | tf_op jit(solution)/shard_map/ppermute | solution.py:22
  145.8 14.1 %collective-permute-start.37 = (f16[128,1024]{1,0:T(8,128)(2,1)S(1)}, f16[128,1024]{1,0:T(8,128)(2,1)S(1)}, u32[]{:S(2)}, u32[]{:S(2)}) collective-permute-start(f16[128,1024]{1,0:T(8,128)(2,1)S(1)} %get-tuple-element.29), channel_id=1, source_target_pairs={{0,4},{2,6},{4,0},{6,2},{1,5},{3,7},{5,1},{7,3},{8,12},{10,14},{12... | collective-permute-start | bytes 786440 | tf_op jit(solution)/shard_map/ppermute | solution.py:22
  171.8 21.7 %collective-permute-start.50 = (bf16[4,128,512]{2,1,0:T(8,128)(2,1)S(1)}, bf16[4,128,512]{2,1,0:T(8,128)(2,1)S(1)}, u32[]{:S(2)}, u32[]{:S(2)}) collective-permute-start(bf16[4,128,512]{2,1,0:T(8,128)(2,1)S(1)} %pad_maximum_fusion.3.refs_8_), channel_id=1, source_target_pairs={{0,8},{8,0},{1,9},{9,1},{2,10},{10,2},{3,11},{11,3},{4,12},{12,4},... | collective-permute-start | bytes 1572872 | tf_op jit(solution)/shard_map/ppermute | solution.py:22
  188.1 13.3 %collective-permute-start.51 = (bf16[4,128,512]{2,1,0:T(8,128)(2,1)S(1)}, bf16[4,128,512]{2,1,0:T(8,128)(2,1)S(1)}, u32[]{:S(2)}, u32[]{:S(2)}) collective-permute-start(bf16[4,128,512]{2,1,0:T(8,128)(2,1)S(1)} %pad_maximum_fusion.3.refs_8_), channel_id=1, source_target_pairs={{0,1},{1,0},{2,3},{3,2},{4,5},{5,4},{6,7},{7,6},{8,9},{9,8},{10,11... | collective-permute-start | bytes 1572872 | tf_op jit(solution)/shard_map/ppermute | solution.py:22
  233.6 19.9 %all-to-all-start.2 = ((bf16[8,2,32,1024]{3,2,1,0:T(8,128)(2,1)}), bf16[8,2,32,1024]{3,2,1,0:T(8,128)(2,1)S(1)}, u32[]{:S(2)}, u32[]{:S(2)}) async-start(bf16[8,2,32,1024]{3,2,1,0:T(8,128)(2,1)} %shard_map.76), calls=%async_computation.2 | async-start | bytes 2097152 | tf_op jit(solution)/shard_map/all_to_all | solution.py:249
  (44 other events, 365.2 us)
